TPU v7x, 128 devices: a whole 4x4x4 slice. The times are simulated.
128 devices in a mesh: head: 2 (over x_lo), page: 64 (over z, y, x_hi, core).
Axes of the slice: x: 4 (x_hi: 2, x_lo: 2; x = x_hi * 2 + x_lo), y: 4, z: 4, core: 2. Of those that a mesh axis runs over, the one named last changes fastest.
Arguments:
- streams: bfloat16 [32768, 4, 2048], P('page', None, 'head'), may hold values from -90 to 90
- hc_read: float32 [4], replicated, may hold values from 0.1 to 0.6
- hc_carry: float32 [4, 4], replicated, may hold values from -1 to 1
- hc_write: float32 [4], replicated, may hold values from 0.5 to 1.5
- w_qkv: bfloat16 [2048, 3, 2048], P(None, None, 'head'), may hold values from -0.125 to 0.125
- w_out: bfloat16 [2048, 2048], P('head'), may hold values from -0.125 to 0.125
- req_lengths: int32 [64, 4], P('page'), may hold values from 1 to 256, 512 in all within a row
- req_age: int32 [64, 4], P('page'), may hold values from 0 to 384
- cache_order: int32 [64, 12], P('page'), may hold values from 0 to 11, each once within a row
- cache_kv: bfloat16 [768, 2, 128, 2048], P('page', None, None, 'head'), may hold values from -240 to 240
- prefill_kv: bfloat16 [256, 1, 2, 128, 2048], P('page', None, None, None, 'head'), may hold values from -6 to 6
- page_table: int32 [256], P('page'), may hold values from 0 to 511, as said below
Outputs:
- new_streams: bfloat16 [32768, 4, 2048], P('page', None, 'head')
- decode_pages: bfloat16 [512, 1, 2, 128, 2048], P('page', None, None, None, 'head')
Inputs may be any that keep to these rules, and one draw needn't show every extreme that they name: `page_table`: distinct values. Block b of page index s goes to owner (s + e) mod 64 with e from 0 to 3; at most 2 blocks of one device go to one owner, and at most 8 blocks to one owner in all; both bounds are reached in every draw.
All inputs are finite; a program needn't handle non-finite values.
Results may differ from a plain program's by a relative error of at most 0.024.
Values may be sent and summed in bfloat16 or wider, within the bound.
No kernel may reach another device: no remote copies, remote signals or barrier semaphores. Data moves between devices by JAX's collectives and lax.ppermute only.
A program may use at most 256 MiB of HBM per device.

v0:
```python
import math

import jax
import jax.numpy as jnp
from jax import lax
from jax.experimental import pallas as pl
from jax.experimental.pallas import tpu as pltpu
from jax.sharding import PartitionSpec as P

F=jnp.float32; B=jnp.bfloat16
NEG=-1e30
def io(shape,d): return lax.broadcasted_iota(jnp.int32,shape,d)
def dot_t(a,b): return lax.dot_general(a,b,(((1,),(1,)),((),())),preferred_element_type=F)
def dot(a,b): return jnp.dot(a,b,preferred_element_type=F)
QSCALE=math.log2(math.e)/math.sqrt(128.0)

def layer_body(len_ref,age_ref,order_ref,head_ref,own_ref,oth_ref,cos_ref,sin_ref,w_hbm,wo_hbm,kv_hbm,keep_ref,send_ref,
               w,wo,kc,vc,nrm,q,k,v,att,s_ref,p_ref,acc,wsem,wosem,csem):
    h=head_ref[0]
    wcp=[pltpu.make_async_copy(w_hbm.at[c],w.at[c],wsem.at[c]) for c in range(3)]
    for c in wcp: c.start()
    ccp=[]
    for i in range(12):
        pg=order_ref[i]
        ccp.append(pltpu.make_async_copy(kv_hbm.at[pg,0],kc.at[pl.ds(i*128,128),:],csem.at[2*i]))
        ccp.append(pltpu.make_async_copy(kv_hbm.at[pg,1],vc.at[pl.ds(i*128,128),:],csem.at[2*i+1]))
    for c in ccp: c.start()
    wocp=pltpu.make_async_copy(wo_hbm,wo,wosem)
    wocp.start()
    hoff=pl.multiple_of(h*1024,1024); ooff=pl.multiple_of((1-h)*1024,1024)
    def ln(i,_):
        r=pl.ds(pl.multiple_of(i*64,64),64)
        a=own_ref[r,:].astype(F); b=oth_ref[r,:].astype(F)
        m=(jnp.sum(a,axis=1,keepdims=True)+jnp.sum(b,axis=1,keepdims=True))*(1.0/2048)
        a=a-m; b=b-m
        var=(jnp.sum(a*a,axis=1,keepdims=True)+jnp.sum(b*b,axis=1,keepdims=True))*(1.0/2048)
        rs=lax.rsqrt(var+1e-5)
        nrm[r,pl.ds(hoff,1024)]=(a*rs).astype(B)
        nrm[r,pl.ds(ooff,1024)]=(b*rs).astype(B)
        return 0
    lax.fori_loop(0,8,ln,0)
    for c,dst in ((0,q),(1,k),(2,v)):
        wcp[c].wait()
        def proj(i,_,c=c,dst=dst):
            col=pl.ds(pl.multiple_of(i*256,256),256)
            for rb in range(2):
                rows=slice(rb*256,rb*256+256)
                x=dot(nrm[rows,:],w[c,:,col])
                if c<2:
                    co=cos_ref[rows,:]; si=sin_ref[rows,:]
                    y=[]
                    for hh in range(2):
                        xh=x[:,hh*128:hh*128+128]
                        z=xh*co+pltpu.roll(xh,64,1)*si
                        if c==0: z=z*QSCALE
                        y.append(z)
                    x=jnp.concatenate(y,axis=1)
                dst[rows,col]=x.astype(B)
            return 0
        lax.fori_loop(0,4,proj,0)
    for c in ccp: c.wait()
    e=[len_ref[0],len_ref[0]+len_ref[1],len_ref[0]+len_ref[1]+len_ref[2]]
    def tile(t,_):
        t0=t*128
        rows=pl.ds(pl.multiple_of(t0,128),128)
        kb=jnp.maximum(t-2,0)*128
        win=pl.ds(pl.multiple_of(kb,128),384)
        ri=t0+io((128,384),0); ki=kb+io((128,384),1)
        st=jnp.where(ri>=e[2],e[2],jnp.where(ri>=e[1],e[1],jnp.where(ri>=e[0],e[0],0)))
        bias=jnp.where((ki>=st)&(ki<=ri),0.0,NEG)
        for hh in range(8):
            hs=slice(hh*128,hh*128+128)
            s_ref[hh,:,384:768]=dot_t(q[rows,hs],k[win,hs])+bias
        rid=t0+io((128,1),0)
        rreq=(rid>=e[0]).astype(jnp.int32)+(rid>=e[1]).astype(jnp.int32)+(rid>=e[2]).astype(jnp.int32)
        last=t0+127
        lo=(t0>=e[0]).astype(jnp.int32)+(t0>=e[1]).astype(jnp.int32)+(t0>=e[2]).astype(jnp.int32)
        hi=(last>=e[0]).astype(jnp.int32)+(last>=e[1]).astype(jnp.int32)+(last>=e[2]).astype(jnp.int32)
        def sc(r,_):
            cb=jnp.where(io((1,384),1)<age_ref[r],0.0,NEG)
            keys=pl.ds(pl.multiple_of(r*384,384),384)
            mine=rreq==r
            for hh in range(8):
                hs=slice(hh*128,hh*128+128)
                x=dot_t(q[rows,hs],kc[keys,hs])+cb
                s_ref[hh,:,0:384]=jnp.where(mine,x,s_ref[hh,:,0:384])
            return 0
        lax.fori_loop(lo,hi+1,sc,0)
        for hh in range(8):
            hs=slice(hh*128,hh*128+128)
            s=s_ref[hh]
            m=jnp.max(s,axis=1,keepdims=True)
            p=jnp.exp2(s-m)
            l=jnp.sum(p,axis=1,keepdims=True)
            p=(p*(1.0/l)).astype(B)
            p_ref[hh]=p[:,0:384]
            acc[:,hs]=dot(p[:,384:768],v[win,hs])
        def pv(r,_):
            keys=pl.ds(pl.multiple_of(r*384,384),384)
            mine=rreq==r
            for hh in range(8):
                hs=slice(hh*128,hh*128+128)
                pm=jnp.where(mine,p_ref[hh],jnp.zeros((),B))
                acc[:,hs]=acc[:,hs]+dot(pm,vc[keys,hs])
            return 0
        lax.fori_loop(lo,hi+1,pv,0)
        att[rows,:]=acc[...].astype(B)
        return 0
    lax.fori_loop(0,4,tile,0)
    wocp.wait()
    def outp(i,_):
        lc=pl.multiple_of(i*256,256)
        for dst,off in ((send_ref,ooff),(keep_ref,hoff)):
            col=pl.ds(pl.multiple_of(off+lc,256),256)
            for rb in range(2):
                rows=slice(rb*256,rb*256+256)
                dst[rows,pl.ds(lc,256)]=dot(att[rows,:],wo[:,col]).astype(B)
        return 0
    lax.fori_loop(0,4,outp,0)

def layer(lens,age,order,head,own,oth,cos,sin,w3,wo,kv):
    vm=pl.BlockSpec(memory_space=pltpu.VMEM); an=pl.BlockSpec(memory_space=pl.ANY); sm=pl.BlockSpec(memory_space=pltpu.SMEM)
    return pl.pallas_call(layer_body,
        out_shape=(jax.ShapeDtypeStruct((512,1024),B),)*2,
        in_specs=[sm]*4+[vm]*4+[an]*3, out_specs=(vm,vm),
        scratch_shapes=[pltpu.VMEM((3,2048,1024),B),pltpu.VMEM((1024,2048),B),pltpu.VMEM((1536,1024),B),pltpu.VMEM((1536,1024),B),
            pltpu.VMEM((512,2048),B),pltpu.VMEM((512,1024),B),pltpu.VMEM((512,1024),B),pltpu.VMEM((512,1024),B),pltpu.VMEM((512,1024),B),
            pltpu.VMEM((8,128,768),F),pltpu.VMEM((8,128,384),B),pltpu.VMEM((128,1024),F),
            pltpu.SemaphoreType.DMA((3,)),pltpu.SemaphoreType.DMA,pltpu.SemaphoreType.DMA((24,))],
        compiler_params=pltpu.CompilerParams(vmem_limit_bytes=60<<20),
        cost_estimate=pl.CostEstimate(flops=14*10**9,bytes_accessed=26<<20,transcendentals=4<<20),
        name='layer')(lens,age,order,head,own,oth,cos,sin,w3,wo,kv)

def tables(lens,age):
    ends=jnp.cumsum(lens); starts=ends-lens
    t=jnp.arange(512,dtype=jnp.int32)
    mem=((t[:,None]>=starts[None,:])&(t[:,None]<ends[None,:])).astype(jnp.int32)
    pos=t+jnp.sum(mem*(age-starts)[None,:],axis=1)
    j=jnp.arange(128,dtype=jnp.int32)
    freq=10000.0**(-2.0*(j%64).astype(F)/128)
    ang=pos.astype(F)[:,None]*freq[None,:]
    return jnp.cos(ang), jnp.where(j[None,:]<64,-1.0,1.0)*jnp.sin(ang)

def rows_view(x):
    return x.reshape(512,4,8,128).transpose(0,2,1,3).reshape(16384,128)

def rows_unview(x):
    return x.reshape(512,8,4,128).transpose(0,2,1,3).reshape(512,4,1024)

NCH=8
TCH=512//NCH

def mix_body(r_ref,x_hbm,o_ref,x,sem):
    cps=[pltpu.make_async_copy(x_hbm.at[pl.ds(c*TCH*32,TCH*32),:],x.at[pl.ds(c*TCH*32,TCH*32),:],sem.at[c]) for c in range(NCH)]
    for c in cps: c.start()
    sh=(64,256); row=io(sh,0); col=io(sh,1)
    c=col&3
    a=jnp.where(c==0,r_ref[0],jnp.where(c==1,r_ref[1],jnp.where(c==2,r_ref[2],r_ref[3])))
    a=jnp.where(((col>>5)==(row&7))&(((col>>2)&7)==(row>>3)),a,0.0)
    hi=a.astype(B)
    A=jnp.concatenate([hi,(a-hi.astype(F)).astype(B)],axis=0)
    for ch in range(NCH):
        cps[ch].wait()
        for g in range(ch*TCH//16,(ch+1)*TCH//16):
            X=jnp.concatenate([x[g*512:g*512+256,:],x[g*512+256:g*512+512,:]],axis=1)
            o=dot(A,X)
            o=o[0:64]+o[64:128]
            for j in range(8):
                o_ref[g*16:g*16+16,j*128:(j+1)*128]=jnp.concatenate([o[j*8:j*8+8,0:128],o[j*8:j*8+8,128:256]],axis=0).astype(B)

def mix(x,r):
    return pl.pallas_call(mix_body,out_shape=jax.ShapeDtypeStruct((512,1024),B),
      in_specs=[pl.BlockSpec(memory_space=pltpu.SMEM),pl.BlockSpec(memory_space=pl.ANY)],
      out_specs=pl.BlockSpec(memory_space=pltpu.VMEM),
      scratch_shapes=[pltpu.VMEM((16384,128),B),pltpu.SemaphoreType.DMA((NCH,))],
      compiler_params=pltpu.CompilerParams(vmem_limit_bytes=60<<20),
      cost_estimate=pl.CostEstimate(flops=10**8,bytes_accessed=6<<20,transcendentals=0),
      name='mix')(r,x)

def fin_body(c_ref,w_ref,x_hbm,a_ref,b_ref,o_hbm,x,o,m_ref,wm_ref,isem,osem):
    icp=[pltpu.make_async_copy(x_hbm.at[pl.ds(c*TCH*32,TCH*32),:],x.at[pl.ds(c*TCH*32,TCH*32),:],isem.at[c]) for c in range(NCH)]
    ocp=[pltpu.make_async_copy(o.at[pl.ds(c*TCH*32,TCH*32),:],o_hbm.at[pl.ds(c*TCH*32,TCH*32),:],osem.at[c]) for c in range(NCH)]
    for c in icp: c.start()
    n=128
    row=io((n,n),0); col=io((n,n),1)
    a=jnp.zeros((n,n),F)
    for i in range(4):
        for j in range(4):
            a=jnp.where(((row&3)==j)&((col&3)==i),c_ref[i*4+j],a)
    a=jnp.where((row>>2)==(col>>2),a,0.0)
    hi=a.astype(B); m_ref[:,0:n]=hi; m_ref[:,n:2*n]=(a-hi.astype(F)).astype(B)
    for s in range(2):
        row=io((n,64),0); col=io((n,64),1)
        a=jnp.zeros((n,64),F)
        for j in range(4): a=jnp.where((row&3)==j,w_ref[j],a)
        a=jnp.where(((row>>5)+s*4==(col&7))&(((row>>2)&7)==(col>>3)),a,0.0)
        hi=a.astype(B); lo=(a-hi.astype(F)).astype(B)
        wm_ref[s*n:(s+1)*n,:]=jnp.concatenate([hi,lo,hi,lo],axis=1)
    M=m_ref[...]
    for ch in range(NCH):
        icp[ch].wait()
        for g in range(ch*TCH//16,(ch+1)*TCH//16):
            def U(ref):
                u=ref[g*16:g*16+16,:].astype(F)
                return jnp.concatenate([jnp.concatenate([u[0:8,j*128:(j+1)*128],u[8:16,j*128:(j+1)*128]],axis=1) for j in range(8)],axis=0).astype(B)
            Ua=U(a_ref);Ub=U(b_ref)
            ou=dot(wm_ref[...],jnp.concatenate([Ua,Ua,Ub,Ub],axis=0))
            r0=g*512
            for s in range(2):
                X=jnp.concatenate([x[r0+s*128:r0+s*128+128,:],x[r0+256+s*128:r0+256+s*128+128,:]],axis=1)
                z=(dot(M,jnp.concatenate([X,X],axis=0))+ou[s*128:(s+1)*128]).astype(B)
                o[r0+s*128:r0+s*128+128,:]=z[:,0:128]; o[r0+256+s*128:r0+256+s*128+128,:]=z[:,128:256]
        ocp[ch].start()
    for c in ocp: c.wait()

def fin(x,u1,u2,cr,w):
    vm=pl.BlockSpec(memory_space=pltpu.VMEM); an=pl.BlockSpec(memory_space=pl.ANY); sm=pl.BlockSpec(memory_space=pltpu.SMEM)
    return pl.pallas_call(fin_body,out_shape=jax.ShapeDtypeStruct((16384,128),B),
      in_specs=[sm,sm,an,vm,vm],out_specs=an,
      scratch_shapes=[pltpu.VMEM((16384,128),B),pltpu.VMEM((16384,128),B),pltpu.VMEM((128,256),B),pltpu.VMEM((256,256),B),
        pltpu.SemaphoreType.DMA((NCH,)),pltpu.SemaphoreType.DMA((NCH,))],
      compiler_params=pltpu.CompilerParams(vmem_limit_bytes=60<<20),
      cost_estimate=pl.CostEstimate(flops=10**9,bytes_accessed=10<<20,transcendentals=0),
      name='fin')(cr,w,x,u1,u2)

def pick_body(tab_ref,me_ref,src,o1,o2,o3,buf,isem,osem):
    me=me_ref[0]
    icp=[pltpu.make_async_copy(src.at[b],buf.at[b],isem.at[b]) for b in range(4)]
    for c in icp: c.start()
    for c in icp: c.wait()
    cps=[]
    for d,dst in ((1,o1),(2,o2),(3,o3)):
        cnt=jnp.int32(0); first=jnp.int32(0); second=jnp.int32(0)
        for b in range(4):
            hit=(((tab_ref[b]>>3)-me)&63)==d
            first=jnp.where(hit&(cnt==0),b,first)
            second=jnp.where(hit&(cnt==1),b,second)
            cnt=cnt+hit.astype(jnp.int32)
        for s,i in ((0,first),(1,second)):
            c=pltpu.make_async_copy(buf.at[i],dst.at[s],osem.at[2*(d-1)+s]); c.start(); cps.append(c)
    for c in cps: c.wait()

def pick(tab,me,pre):
    an=pl.BlockSpec(memory_space=pl.ANY); sm=pl.BlockSpec(memory_space=pltpu.SMEM)
    return pl.pallas_call(pick_body,out_shape=(jax.ShapeDtypeStruct((2,2,128,1024),B),)*3,
      in_specs=[sm,sm,an],out_specs=(an,)*3,scratch_shapes=[pltpu.VMEM((4,2,128,1024),B),pltpu.SemaphoreType.DMA((4,)),pltpu.SemaphoreType.DMA((6,))],
      compiler_params=pltpu.CompilerParams(vmem_limit_bytes=60<<20),
      cost_estimate=pl.CostEstimate(flops=0,bytes_accessed=6<<20,transcendentals=0),
      name='pick')(tab,me,pre)

def place_body(t0,t1,t2,t3,me_ref,src,r1,r2,r3,out,buf,zero,isem,osem):
    me=me_ref[0]
    used=jnp.int32(0)
    for tab,ref,own in ((t0,src,True),(t1,r1,False),(t2,r2,False),(t3,r3,False)):
        cnt=jnp.int32(0)
        for b in range(4):
            v=tab[b]
            hit=(v>>3)==me
            slot=v&7
            i=b if own else jnp.minimum(cnt,1)
            @pl.when(hit)
            def _(ref=ref,i=i,slot=slot):
                pltpu.make_async_copy(ref.at[i],buf.at[slot],isem.at[slot]).start()
            cnt=cnt+hit.astype(jnp.int32)
            used=used|jnp.where(hit,jnp.int32(1)<<slot,0)
    zero[...]=jnp.zeros_like(zero)
    for s in range(8):
        @pl.when(((used>>s)&1)==0)
        def _(s=s):
            pltpu.make_async_copy(zero,out.at[s],osem.at[s]).start()
    for s in range(8):
        @pl.when(((used>>s)&1)==1)
        def _(s=s):
            pltpu.make_async_copy(src.at[0],buf.at[s],isem.at[s]).wait()
            pltpu.make_async_copy(buf.at[s],out.at[s],osem.at[s]).start()
    for s in range(8):
        pltpu.make_async_copy(zero,out.at[s],osem.at[s]).wait()

def place(tabs,me,pre,r1,r2,r3):
    an=pl.BlockSpec(memory_space=pl.ANY); sm=pl.BlockSpec(memory_space=pltpu.SMEM)
    return pl.pallas_call(place_body,out_shape=jax.ShapeDtypeStruct((8,2,128,1024),B),
      in_specs=[sm]*5+[an]*4,out_specs=an,
      scratch_shapes=[pltpu.VMEM((8,2,128,1024),B),pltpu.VMEM((2,128,1024),B),pltpu.SemaphoreType.DMA((8,)),pltpu.SemaphoreType.DMA((8,))],
      compiler_params=pltpu.CompilerParams(vmem_limit_bytes=60<<20),
      cost_estimate=pl.CostEstimate(flops=0,bytes_accessed=8<<20,transcendentals=0),
      name='place')(*tabs,me,pre,r1,r2,r3)

def ahead(value,steps):
    return lax.ppermute(value,"page",[(s,(s+steps)%64) for s in range(64)])

def swap(value):
    return lax.ppermute(value,"head",[(0,1),(1,0)])

def body(streams,hc_read,hc_carry,hc_write,w_qkv,w_out,req_lengths,req_age,cache_order,cache_kv,prefill_kv,page_table):
    head=lax.axis_index("head").astype(jnp.int32).reshape(1)
    me=lax.axis_index("page").astype(jnp.int32).reshape(1)
    lens=req_lengths[0]; age=req_age[0]; order=cache_order[0]
    x=rows_view(streams)
    own=mix(x,hc_read)
    oth=swap(own)
    pre=prefill_kv.reshape(4,2,128,1024)
    table=page_table
    own_dep,table_dep=lax.optimization_barrier((own,table))
    s1,s2,s3=pick(table_dep,me,pre)
    r1=ahead(s1,1); r2=ahead(s2,2); r3=ahead(s3,3)
    tabs=(table,ahead(table,1),ahead(table,2),ahead(table,3))
    cos,sin=tables(lens,age)
    oth,tabs=lax.optimization_barrier((oth,tabs))
    w3=w_qkv.transpose(1,0,2)
    keep,send=layer(lens,age,order,head,own,oth,cos,sin,w3,w_out,cache_kv)
    recv=swap(send)
    pages=place(tabs,me,pre,r1,r2,r3)
    carry=(jnp.eye(4,dtype=F)+hc_carry).reshape(16)
    new=fin(x,keep,recv,carry,hc_write)
    return rows_unview(new),pages.reshape(8,1,2,128,1024)

def solution(mesh):
    placed=(P("page",None,"head"),P(),P(),P(),P(None,None,"head"),P("head",None),P("page",None),P("page",None),P("page",None),
        P("page",None,None,"head"),P("page",None,None,None,"head"),P("page"))
    return jax.shard_map(body,mesh=mesh,in_specs=placed,out_specs=(P("page",None,"head"),P("page",None,None,None,"head")),check_vma=False)
```

profile of v0, /device:TPU:1, one launch (start us, length us, event | category | flops | bytes accessed | tf_op | source)
XLA Modules:
  0.0 105.5 jit_solution(9432726107701475757)
XLA Ops:
  0.6 0.0 copy-start.4
  0.6 0.0 copy-start.5
  0.7 0.0 copy-start.6
  0.7 4.8 %mix.1.own_ref = bf16[512,1024]{1,0:T(8,128)(2,1)} custom-call(f32[4]{0:T(128)} %r_ref.1, bf16[16384,128]{1,0:T(8,128)(2,1)} %bitcast.32), custom_call_target="tpu_custom_call" | custom-call | flops 100000000 | bytes 6291456 | tf_op jit(solution)/shard_map/mix/pallas_call | solution.py:172
  5.4 2.1 %collective-permute-start = (bf16[512,1024]{1,0:T(8,128)(2,1)}, bf16[512,1024]{1,0:T(8,128)(2,1)}, u32[]{:S(2)}, u32[]{:S(2)}) collective-permute-start(bf16[512,1024]{1,0:T(8,128)(2,1)} %mix.1.own_ref), channel_id=1, source_target_pairs={{0,64},{64,0},{1,65},{65,1},{2,66},{66,2},{3,67},{67,3},{4,68},{68... | collective-permute-start | bytes 3145736 | tf_op jit(solution)/shard_map/ppermute | solution.py:292
  7.6 0.0 copy-done.4
  7.6 2.1 %collective-permute-start.3 = (s32[4]{0:T(128)S(1)}, s32[4]{0:T(128)S(1)}, u32[]{:S(2)}, u32[]{:S(2)}) collective-permute-start(s32[4]{0:T(128)S(1)} %copy-done.4), channel_id=1, source_target_pairs={{0,3},{1,4},{2,5},{3,6},{4,7},{5,8},{6,9},{7,10},{8,11},{9,12},{10... | collective-permute-start | bytes 56 | tf_op jit(solution)/shard_map/ppermute | solution.py:289
  9.7 2.5 %collective-permute-start.2 = (s32[4]{0:T(128)S(1)}, s32[4]{0:T(128)S(1)}, u32[]{:S(2)}, u32[]{:S(2)}) collective-permute-start(s32[4]{0:T(128)S(1)} %copy-done.4), channel_id=1, source_target_pairs={{0,2},{1,3},{2,4},{3,5},{4,6},{5,7},{6,8},{7,9},{8,10},{9,11},{10,... | collective-permute-start | bytes 56 | tf_op jit(solution)/shard_map/ppermute | solution.py:289
  12.2 2.4 %collective-permute-start.1 = (s32[4]{0:T(128)S(1)}, s32[4]{0:T(128)S(1)}, u32[]{:S(2)}, u32[]{:S(2)}) collective-permute-start(s32[4]{0:T(128)S(1)} %copy-done.4), channel_id=1, source_target_pairs={{0,1},{1,2},{2,3},{3,4},{4,5},{5,6},{6,7},{7,8},{8,9},{9,10},{10,1... | collective-permute-start | bytes 56 | tf_op jit(solution)/shard_map/ppermute | solution.py:289
  14.6 4.0 %pick.1 = (bf16[2,2,128,1024]{3,2,1,0:T(8,128)(2,1)}, bf16[2,2,128,1024]{3,2,1,0:T(8,128)(2,1)}, bf16[2,2,128,1024]{3,2,1,0:T(8,128)(2,1)}) custom-call(s32[4]{0:T(128)} %t0, s32[1]{0:T(128)} %bitcast.18.me_ref, bf16[4,2,128,1024]{3,2,1,0:T(8,128)(2,1)} %bitcast.34), custom_call_target="tpu_custom_call" | custom-call | bytes 6291456 | tf_op jit(solution)/shard_map/pick/pallas_call | solution.py:245
  18.5 0.1 collective-permute-start.5
  18.6 0.2 reduce-window.4
  18.8 0.1 select_reduce_fusion
  18.9 1.8 %fusion = (f32[512,128]{1,0:T(8,128)}, f32[512,128]{1,0:T(8,128)}) fusion(f32[128]{0:T(128)S(1)} %get-tuple-element.32, f32[128]{0:T(128)S(1)} %get-tuple-element.33, f32[512]{0:T(512)S(1)} %add_convert_fusion), kind=kLoop, calls=%fused_computation.2 | loop fusion | flops 131072 | bytes 527360 | tf_op jit(solution)/shard_map/mul | solution.py:142
  20.8 20.2 %collective-permute-done.3.t3 = s32[4]{0:T(128)S(1)} collective-permute-done((s32[4]{0:T(128)S(1)}, s32[4]{0:T(128)S(1)}, u32[]{:S(2)}, u32[]{:S(2)}) %collective-permute-start.3) | collective-permute-done | bytes 48 | tf_op jit(solution)/shard_map/ppermute | solution.py:289
  41.0 0.0 collective-permute-start.6
  41.0 0.0 collective-permute-done.2.t2
  41.0 0.1 collective-permute-start.7
  41.1 0.0 collective-permute-done.1.t1
  41.1 0.0 copy-start.9
  41.1 0.0 collective-permute-done.oth_ref
  41.1 0.0 copy-start.3
  41.1 31.3 %layer.1 = (bf16[512,1024]{1,0:T(8,128)(2,1)}, bf16[512,1024]{1,0:T(8,128)(2,1)}) custom-call(s32[4]{0:T(128)} %bitcast.39, s32[4]{0:T(128)} %bitcast.41, s32[12]{0:T(128)} %bitcast.43, s32[1]{0:T(128)} %bitcast.6.head_ref, bf16[512,1024]{1,0:T(8,128)(2,1)} %mix.1.own_ref, bf16[512,1024]{1,0:T(8,128)(2,1)} %collective-permute-done.oth_ref, ...), custom_call_target="tpu_custom_call" | custom-call | flops 14000000000 | bytes 27262976 | tf_op jit(solution)/shard_map/layer/pallas_call | solution.py:123
  72.5 0.3 collective-permute-start.4
  72.8 0.6 reshape.68.c_ref
  73.4 0.0 collective-permute-done.5.r1
  73.4 8.7 %collective-permute-done.6.r2 = bf16[2,2,128,1024]{3,2,1,0:T(8,128)(2,1)S(1)} collective-permute-done((bf16[2,2,128,1024]{3,2,1,0:T(8,128)(2,1)}, bf16[2,2,128,1024]{3,2,1,0:T(8,128)(2,1)S(1)}, u32[]{:S(2)}, u32[]{:S(2)}) %collective-permute-start.6) | collective-permute-done | bytes 1048608 | tf_op jit(solution)/shard_map/ppermute | solution.py:289
  82.0 7.2 %collective-permute-done.7.r3 = bf16[2,2,128,1024]{3,2,1,0:T(8,128)(2,1)S(1)} collective-permute-done((bf16[2,2,128,1024]{3,2,1,0:T(8,128)(2,1)}, bf16[2,2,128,1024]{3,2,1,0:T(8,128)(2,1)S(1)}, u32[]{:S(2)}, u32[]{:S(2)}) %collective-permute-start.7) | collective-permute-done | bytes 1048608 | tf_op jit(solution)/shard_map/ppermute | solution.py:289
  89.2 1.0 copy-done.2
  90.2 4.4 %place.1 = bf16[8,2,128,1024]{3,2,1,0:T(8,128)(2,1)} custom-call(s32[4]{0:T(128)} %t0, s32[4]{0:T(128)} %copy-done.9, s32[4]{0:T(128)} %copy-done.8, s32[4]{0:T(128)} %copy-done.7, s32[1]{0:T(128)} %bitcast.18.me_ref, bf16[4,2,128,1024]{3,2,1,0:T(8,128)(2,1)} %bitcast.35, bf16[2,2,128,1024]{3,2,1,0:T(8,128)(2,1)} %copy-done, ...), custom_call_target="tpu_custom_call" | custom-call | bytes 8388608 | tf_op jit(solution)/shard_map/place/pallas_call | solution.py:281
  94.6 3.6 %collective-permute-done.4.b_ref = bf16[512,1024]{1,0:T(8,128)(2,1)} collective-permute-done((bf16[512,1024]{1,0:T(8,128)(2,1)}, bf16[512,1024]{1,0:T(8,128)(2,1)}, u32[]{:S(2)}, u32[]{:S(2)}) %collective-permute-start.4) | collective-permute-done | bytes 1048608 | tf_op jit(solution)/shard_map/ppermute | solution.py:292
  98.3 7.1 %fin.1 = bf16[16384,128]{1,0:T(8,128)(2,1)} custom-call(f32[16]{0:T(128)} %reshape.68.c_ref, f32[4]{0:T(128)} %w_ref.1, bf16[16384,128]{1,0:T(8,128)(2,1)} %bitcast.33, bf16[512,1024]{1,0:T(8,128)(2,1)} %get-tuple-element.14.a_ref, bf16[512,1024]{1,0:T(8,128)(2,1)} %collective-permute-done.4.b_ref), custom_call_target="tpu_custom_call" | custom-call | flops 1000000000 | bytes 10485760 | tf_op jit(solution)/shard_map/fin/pallas_call | solution.py:218
  (17 shorter events, 0.1 us)
Async XLA Ops:
  0.6 6.9 %copy-start.4 = (s32[4]{0:T(128)S(1)}, s32[4]{0:T(128)}, u32[]{:S(2)}) copy-start(s32[4]{0:T(128)} %t0) | copy-start | bytes 52
  0.6 18.0 %copy-start.5 = (s32[1,4]{1,0:T(1,128)S(1)}, s32[1,4]{1,0:T(1,128)}, u32[]{:S(2)}) copy-start(s32[1,4]{1,0:T(1,128)} %param.18) | copy-start | bytes 52
  0.7 18.2 %copy-start.6 = (s32[1,4]{1,0:T(1,128)S(1)}, s32[1,4]{1,0:T(1,128)}, u32[]{:S(2)}) copy-start(s32[1,4]{1,0:T(1,128)} %param.19) | copy-start | bytes 52
  5.4 35.7 %collective-permute-start = (bf16[512,1024]{1,0:T(8,128)(2,1)}, bf16[512,1024]{1,0:T(8,128)(2,1)}, u32[]{:S(2)}, u32[]{:S(2)}) collective-permute-start(bf16[512,1024]{1,0:T(8,128)(2,1)} %mix.1.own_ref), channel_id=1, source_target_pairs={{0,64},{64,0},{1,65},{65,1},{2,66},{66,2},{3,67},{67,3},{4,68},{68... | collective-permute-start | bytes 3145736 | tf_op jit(solution)/shard_map/ppermute | solution.py:292
  7.6 33.4 %collective-permute-start.3 = (s32[4]{0:T(128)S(1)}, s32[4]{0:T(128)S(1)}, u32[]{:S(2)}, u32[]{:S(2)}) collective-permute-start(s32[4]{0:T(128)S(1)} %copy-done.4), channel_id=1, source_target_pairs={{0,3},{1,4},{2,5},{3,6},{4,7},{5,8},{6,9},{7,10},{8,11},{9,12},{10... | collective-permute-start | bytes 56 | tf_op jit(solution)/shard_map/ppermute | solution.py:289
  9.7 31.3 %collective-permute-start.2 = (s32[4]{0:T(128)S(1)}, s32[4]{0:T(128)S(1)}, u32[]{:S(2)}, u32[]{:S(2)}) collective-permute-start(s32[4]{0:T(128)S(1)} %copy-done.4), channel_id=1, source_target_pairs={{0,2},{1,3},{2,4},{3,5},{4,6},{5,7},{6,8},{7,9},{8,10},{9,11},{10,... | collective-permute-start | bytes 56 | tf_op jit(solution)/shard_map/ppermute | solution.py:289
  12.2 28.9 %collective-permute-start.1 = (s32[4]{0:T(128)S(1)}, s32[4]{0:T(128)S(1)}, u32[]{:S(2)}, u32[]{:S(2)}) collective-permute-start(s32[4]{0:T(128)S(1)} %copy-done.4), channel_id=1, source_target_pairs={{0,1},{1,2},{2,3},{3,4},{4,5},{5,6},{6,7},{7,8},{8,9},{9,10},{10,1... | collective-permute-start | bytes 56 | tf_op jit(solution)/shard_map/ppermute | solution.py:289
  18.5 54.8 %collective-permute-start.5 = (bf16[2,2,128,1024]{3,2,1,0:T(8,128)(2,1)}, bf16[2,2,128,1024]{3,2,1,0:T(8,128)(2,1)S(1)}, u32[]{:S(2)}, u32[]{:S(2)}) collective-permute-start(bf16[2,2,128,1024]{3,2,1,0:T(8,128)(2,1)} %get-tuple-element.21), channel_id=1, source_target_pairs={{0,1},{1,2},{2,3},{3,4},{4,5},{5,6},{6,7},{7,8},{8,9},{9,10},{10,1... | collective-permute-start | bytes 3145736 | tf_op jit(solution)/shard_map/ppermute | solution.py:289
  41.0 31.4 %copy-start.7 = (s32[4]{0:T(128)}, s32[4]{0:T(128)S(1)}, u32[]{:S(2)}) copy-start(s32[4]{0:T(128)S(1)} %collective-permute-done.3.t3) | copy-start | bytes 52
  41.0 41.0 %collective-permute-start.6 = (bf16[2,2,128,1024]{3,2,1,0:T(8,128)(2,1)}, bf16[2,2,128,1024]{3,2,1,0:T(8,128)(2,1)S(1)}, u32[]{:S(2)}, u32[]{:S(2)}) collective-permute-start(bf16[2,2,128,1024]{3,2,1,0:T(8,128)(2,1)} %get-tuple-element.22), channel_id=1, source_target_pairs={{0,2},{1,3},{2,4},{3,5},{4,6},{5,7},{6,8},{7,9},{8,10},{9,11},{10,... | collective-permute-start | bytes 3145736 | tf_op jit(solution)/shard_map/ppermute | solution.py:289
  41.0 31.4 %copy-start.8 = (s32[4]{0:T(128)}, s32[4]{0:T(128)S(1)}, u32[]{:S(2)}) copy-start(s32[4]{0:T(128)S(1)} %collective-permute-done.2.t2) | copy-start | bytes 52
  41.0 48.2 %collective-permute-start.7 = (bf16[2,2,128,1024]{3,2,1,0:T(8,128)(2,1)}, bf16[2,2,128,1024]{3,2,1,0:T(8,128)(2,1)S(1)}, u32[]{:S(2)}, u32[]{:S(2)}) collective-permute-start(bf16[2,2,128,1024]{3,2,1,0:T(8,128)(2,1)} %get-tuple-element.23), channel_id=1, source_target_pairs={{0,3},{1,4},{2,5},{3,6},{4,7},{5,8},{6,9},{7,10},{8,11},{9,12},{10... | collective-permute-start | bytes 3145736 | tf_op jit(solution)/shard_map/ppermute | solution.py:289
  41.1 31.4 %copy-start.9 = (s32[4]{0:T(128)}, s32[4]{0:T(128)S(1)}, u32[]{:S(2)}) copy-start(s32[4]{0:T(128)S(1)} %collective-permute-done.1.t1) | copy-start | bytes 52
  41.1 31.6 %copy-start.3 = (f32[4,4]{1,0:T(4,128)S(1)}, f32[4,4]{1,0:T(4,128)}, u32[]{:S(2)}) copy-start(f32[4,4]{1,0:T(4,128)} %param.14) | copy-start | bytes 196
  72.5 25.8 %collective-permute-start.4 = (bf16[512,1024]{1,0:T(8,128)(2,1)}, bf16[512,1024]{1,0:T(8,128)(2,1)}, u32[]{:S(2)}, u32[]{:S(2)}) collective-permute-start(bf16[512,1024]{1,0:T(8,128)(2,1)} %get-tuple-element.15), channel_id=1, source_target_pairs={{0,64},{64,0},{1,65},{65,1},{2,66},{66,2},{3,67},{67,3},{4,68},{68... | collective-permute-start | bytes 3145736 | tf_op jit(solution)/shard_map/ppermute | solution.py:292
  73.4 15.9 %copy-start = (bf16[2,2,128,1024]{3,2,1,0:T(8,128)(2,1)}, bf16[2,2,128,1024]{3,2,1,0:T(8,128)(2,1)S(1)}, u32[]{:S(2)}) copy-start(bf16[2,2,128,1024]{3,2,1,0:T(8,128)(2,1)S(1)} %collective-permute-done.5.r1) | copy-start | bytes 3145732
  82.0 7.2 %copy-start.1 = (bf16[2,2,128,1024]{3,2,1,0:T(8,128)(2,1)}, bf16[2,2,128,1024]{3,2,1,0:T(8,128)(2,1)S(1)}, u32[]{:S(2)}) copy-start(bf16[2,2,128,1024]{3,2,1,0:T(8,128)(2,1)S(1)} %collective-permute-done.6.r2) | copy-start | bytes 3145732
  89.2 1.0 copy-start.2
where the time goes:
time: 107 us; the launch traced here: 106 us
  Pallas kernels  51.5 us (48%)
  waiting for transfers between devices  39.7 us (37%)
  starting transfers between devices  9.53 us (9%)
  other arithmetic  2.14 us (2%)
  local copies, waits for them, and re-layouts  1.65 us (2%)
    ppermute x6, waiting for transfers between devices, ahead(): lax.ppermute(value, 'page', [(s, (s + steps) % 64) for s in range(64)])  36.1 us
    pallas_call x1, Pallas kernels, layer(): pl.pallas_call(layer_body, out_shape=(jax.ShapeDtypeStruct((512, 1024), B...  31.3 us
    ppermute x6, starting transfers between devices, ahead(): lax.ppermute(value, 'page', [(s, (s + steps) % 64) for s in range(64)])  7.14 us
    pallas_call x1, Pallas kernels, fin(): pl.pallas_call(fin_body, out_shape=jax.ShapeDtypeStruct((16384, 128), B),...  7.07 us
    pallas_call x1, Pallas kernels, mix(): pl.pallas_call(mix_body, out_shape=jax.ShapeDtypeStruct((512, 1024), B),...  4.78 us
    pallas_call x1, Pallas kernels, place(): pl.pallas_call(place_body, out_shape=jax.ShapeDtypeStruct((8, 2, 128, 102...  4.4 us
    pallas_call x1, Pallas kernels, pick(): pl.pallas_call(pick_body, out_shape=(jax.ShapeDtypeStruct((2, 2, 128, 102...  3.97 us
    ppermute x2, waiting for transfers between devices, swap(): return lax.ppermute(value, 'head', [(0, 1), (1, 0)])  3.65 us
  transfers between devices with their start and end apart: 8, of which 4 were waited for; matrix products, arithmetic and copies ran while one was open for 3% of the time, Pallas kernels for 38%

commit v1 on v0

--- a/solution.py
+++ b/solution.py
@@ -127,7 +127,7 @@
             pltpu.VMEM((512,2048),B),pltpu.VMEM((512,1024),B),pltpu.VMEM((512,1024),B),pltpu.VMEM((512,1024),B),pltpu.VMEM((512,1024),B),
             pltpu.VMEM((8,128,768),F),pltpu.VMEM((8,128,384),B),pltpu.VMEM((128,1024),F),
             pltpu.SemaphoreType.DMA((3,)),pltpu.SemaphoreType.DMA,pltpu.SemaphoreType.DMA((24,))],
-        compiler_params=pltpu.CompilerParams(vmem_limit_bytes=60<<20),
+        compiler_params=pltpu.CompilerParams(vmem_limit_bytes=48<<20),
         cost_estimate=pl.CostEstimate(flops=14*10**9,bytes_accessed=26<<20,transcendentals=4<<20),
         name='layer')(lens,age,order,head,own,oth,cos,sin,w3,wo,kv)
 
@@ -173,7 +173,7 @@
       in_specs=[pl.BlockSpec(memory_space=pltpu.SMEM),pl.BlockSpec(memory_space=pl.ANY)],
       out_specs=pl.BlockSpec(memory_space=pltpu.VMEM),
       scratch_shapes=[pltpu.VMEM((16384,128),B),pltpu.SemaphoreType.DMA((NCH,))],
-      compiler_params=pltpu.CompilerParams(vmem_limit_bytes=60<<20),
+      compiler_params=pltpu.CompilerParams(vmem_limit_bytes=61<<20),
       cost_estimate=pl.CostEstimate(flops=10**8,bytes_accessed=6<<20,transcendentals=0),
       name='mix')(r,x)
 
@@ -219,49 +219,66 @@
       in_specs=[sm,sm,an,vm,vm],out_specs=an,
       scratch_shapes=[pltpu.VMEM((16384,128),B),pltpu.VMEM((16384,128),B),pltpu.VMEM((128,256),B),pltpu.VMEM((256,256),B),
         pltpu.SemaphoreType.DMA((NCH,)),pltpu.SemaphoreType.DMA((NCH,))],
-      compiler_params=pltpu.CompilerParams(vmem_limit_bytes=60<<20),
+      compiler_params=pltpu.CompilerParams(vmem_limit_bytes=61<<20),
       cost_estimate=pl.CostEstimate(flops=10**9,bytes_accessed=10<<20,transcendentals=0),
       name='fin')(cr,w,x,u1,u2)
 
-def pick_body(tab_ref,me_ref,src,o1,o2,o3,buf,isem,osem):
+PAY=528
+
+def pick_body(tab_ref,me_ref,src,o1,o2,o3,buf,lab,isem,osem):
     me=me_ref[0]
-    icp=[pltpu.make_async_copy(src.at[b],buf.at[b],isem.at[b]) for b in range(4)]
+    icp=[pltpu.make_async_copy(src.at[pl.ds(b*256,256),:],buf.at[b],isem.at[b]) for b in range(4)]
     for c in icp: c.start()
+    plan=[]
+    for d,dst in ((3,o3),(2,o2),(1,o1)):
+        cnt=jnp.int32(0); i=[jnp.int32(0)]*2; l=[jnp.int32(-1)]*2
+        for b in range(4):
+            hit=(((tab_ref[b]>>3)-me)&63)==d
+            for s in range(2):
+                i[s]=jnp.where(hit&(cnt==s),b,i[s])
+                l[s]=jnp.where(hit&(cnt==s),tab_ref[b]&7,l[s])
+            cnt=cnt+hit.astype(jnp.int32)
+        lab[d-1]=jnp.where(io((16,1024),0)<8,l[0].astype(F),l[1].astype(F)).astype(B)
+        plan.append((d,dst,i))
     for c in icp: c.wait()
     cps=[]
-    for d,dst in ((1,o1),(2,o2),(3,o3)):
-        cnt=jnp.int32(0); first=jnp.int32(0); second=jnp.int32(0)
-        for b in range(4):
-            hit=(((tab_ref[b]>>3)-me)&63)==d
-            first=jnp.where(hit&(cnt==0),b,first)
-            second=jnp.where(hit&(cnt==1),b,second)
-            cnt=cnt+hit.astype(jnp.int32)
-        for s,i in ((0,first),(1,second)):
-            c=pltpu.make_async_copy(buf.at[i],dst.at[s],osem.at[2*(d-1)+s]); c.start(); cps.append(c)
+    for d,dst,i in plan:
+        for s in range(2):
+            cps.append(pltpu.make_async_copy(buf.at[i[s]],dst.at[pl.ds(s*256,256),:],osem.at[3*(d-1)+s]))
+        cps.append(pltpu.make_async_copy(lab.at[d-1],dst.at[pl.ds(512,16),:],osem.at[3*(d-1)+2]))
+    for c in cps: c.start()
     for c in cps: c.wait()
 
 def pick(tab,me,pre):
     an=pl.BlockSpec(memory_space=pl.ANY); sm=pl.BlockSpec(memory_space=pltpu.SMEM)
-    return pl.pallas_call(pick_body,out_shape=(jax.ShapeDtypeStruct((2,2,128,1024),B),)*3,
-      in_specs=[sm,sm,an],out_specs=(an,)*3,scratch_shapes=[pltpu.VMEM((4,2,128,1024),B),pltpu.SemaphoreType.DMA((4,)),pltpu.SemaphoreType.DMA((6,))],
-      compiler_params=pltpu.CompilerParams(vmem_limit_bytes=60<<20),
+    return pl.pallas_call(pick_body,out_shape=(jax.ShapeDtypeStruct((PAY,1024),B),)*3,
+      in_specs=[sm,sm,an],out_specs=(an,)*3,
+      scratch_shapes=[pltpu.VMEM((4,256,1024),B),pltpu.VMEM((3,16,1024),B),pltpu.SemaphoreType.DMA((4,)),pltpu.SemaphoreType.DMA((9,))],
+      compiler_params=pltpu.CompilerParams(vmem_limit_bytes=61<<20),
       cost_estimate=pl.CostEstimate(flops=0,bytes_accessed=6<<20,transcendentals=0),
       name='pick')(tab,me,pre)
 
-def place_body(t0,t1,t2,t3,me_ref,src,r1,r2,r3,out,buf,zero,isem,osem):
+def place_body(tab,me_ref,src,r1,r2,r3,out,buf,zero,lab,lsem,isem,osem):
     me=me_ref[0]
     used=jnp.int32(0)
-    for tab,ref,own in ((t0,src,True),(t1,r1,False),(t2,r2,False),(t3,r3,False)):
-        cnt=jnp.int32(0)
-        for b in range(4):
-            v=tab[b]
-            hit=(v>>3)==me
+    lcp=[pltpu.make_async_copy(r.at[pl.ds(512,16),:],lab.at[d],lsem.at[d]) for d,r in enumerate((r1,r2,r3))]
+    for c in lcp: c.start()
+    def fetch(hit,ref,start,slot):
+        @pl.when(hit)
+        def _():
+            pltpu.make_async_copy(ref.at[pl.ds(start,256),:],buf.at[slot],isem.at[slot]).start()
+    for b in range(4):
+        hit=(tab[b]>>3)==me
+        slot=tab[b]&7
+        fetch(hit,src,b*256,slot)
+        used=used|jnp.where(hit,jnp.int32(1)<<slot,0)
+    for d,ref in enumerate((r1,r2,r3)):
+        lcp[d].wait()
+        for s in range(2):
+            v=jnp.max(lab[d,:,0:128].astype(F)[s*8:s*8+8]).astype(jnp.int32)
+            hit=v>=0
             slot=v&7
-            i=b if own else jnp.minimum(cnt,1)
-            @pl.when(hit)
-            def _(ref=ref,i=i,slot=slot):
-                pltpu.make_async_copy(ref.at[i],buf.at[slot],isem.at[slot]).start()
-            cnt=cnt+hit.astype(jnp.int32)
+            fetch(hit,ref,s*256,slot)
             used=used|jnp.where(hit,jnp.int32(1)<<slot,0)
     zero[...]=jnp.zeros_like(zero)
     for s in range(8):
@@ -271,19 +288,20 @@
     for s in range(8):
         @pl.when(((used>>s)&1)==1)
         def _(s=s):
-            pltpu.make_async_copy(src.at[0],buf.at[s],isem.at[s]).wait()
+            pltpu.make_async_copy(src.at[pl.ds(0,256),:],buf.at[s],isem.at[s]).wait()
             pltpu.make_async_copy(buf.at[s],out.at[s],osem.at[s]).start()
     for s in range(8):
         pltpu.make_async_copy(zero,out.at[s],osem.at[s]).wait()
 
-def place(tabs,me,pre,r1,r2,r3):
+def place(tab,me,pre,r1,r2,r3):
     an=pl.BlockSpec(memory_space=pl.ANY); sm=pl.BlockSpec(memory_space=pltpu.SMEM)
-    return pl.pallas_call(place_body,out_shape=jax.ShapeDtypeStruct((8,2,128,1024),B),
-      in_specs=[sm]*5+[an]*4,out_specs=an,
-      scratch_shapes=[pltpu.VMEM((8,2,128,1024),B),pltpu.VMEM((2,128,1024),B),pltpu.SemaphoreType.DMA((8,)),pltpu.SemaphoreType.DMA((8,))],
-      compiler_params=pltpu.CompilerParams(vmem_limit_bytes=60<<20),
+    return pl.pallas_call(place_body,out_shape=jax.ShapeDtypeStruct((8,256,1024),B),
+      in_specs=[sm]*2+[an]*4,out_specs=an,
+      scratch_shapes=[pltpu.VMEM((8,256,1024),B),pltpu.VMEM((256,1024),B),pltpu.VMEM((3,16,1024),B),
+        pltpu.SemaphoreType.DMA((3,)),pltpu.SemaphoreType.DMA((8,)),pltpu.SemaphoreType.DMA((8,))],
+      compiler_params=pltpu.CompilerParams(vmem_limit_bytes=61<<20),
       cost_estimate=pl.CostEstimate(flops=0,bytes_accessed=8<<20,transcendentals=0),
-      name='place')(*tabs,me,pre,r1,r2,r3)
+      name='place')(tab,me,pre,r1,r2,r3)
 
 def ahead(value,steps):
     return lax.ppermute(value,"page",[(s,(s+steps)%64) for s in range(64)])
@@ -298,18 +316,18 @@
     x=rows_view(streams)
     own=mix(x,hc_read)
     oth=swap(own)
-    pre=prefill_kv.reshape(4,2,128,1024)
-    table=page_table
-    own_dep,table_dep=lax.optimization_barrier((own,table))
-    s1,s2,s3=pick(table_dep,me,pre)
-    r1=ahead(s1,1); r2=ahead(s2,2); r3=ahead(s3,3)
-    tabs=(table,ahead(table,1),ahead(table,2),ahead(table,3))
+    pre=prefill_kv.reshape(1024,1024)
+    own_dep,table=lax.optimization_barrier((own,page_table))
+    s1,s2,s3=pick(table,me,pre)
+    r3=ahead(s3,3)
     cos,sin=tables(lens,age)
-    oth,tabs=lax.optimization_barrier((oth,tabs))
+    oth,s1,s2=lax.optimization_barrier((oth,s1,s2))
+    r2=ahead(s2,2); r1=ahead(s1,1)
     w3=w_qkv.transpose(1,0,2)
     keep,send=layer(lens,age,order,head,own,oth,cos,sin,w3,w_out,cache_kv)
     recv=swap(send)
-    pages=place(tabs,me,pre,r1,r2,r3)
+    pages=place(page_table,me,pre,r1,r2,r3)
+    recv,pages=lax.optimization_barrier((recv,pages))
     carry=(jnp.eye(4,dtype=F)+hc_carry).reshape(16)
     new=fin(x,keep,recv,carry,hc_write)
     return rows_unview(new),pages.reshape(8,1,2,128,1024)

time: 107 us -> 108 us (level); the launches traced: 106 us -> 108 us
  waiting for transfers between devices: 39.7 us -> 42.4 us
  Pallas kernels: 51.5 us -> 49.6 us
  starting transfers between devices: 9.53 us -> 11.3 us
    ppermute x2, waiting for transfers between devices: 3.65 us -> 23.3 us  [swap(): return lax.ppermute(value, 'head', [(0, 1), (1, 0)])]
    ppermute x6 -> x3, waiting for transfers between devices: 36.1 us -> 19.1 us  [ahead(): lax.ppermute(value, 'page', [(s, (s + steps) % 64) for s in range(64)])]
    pallas_call x1, Pallas kernels: 31.3 us -> 29 us  [layer(): pl.pallas_call(layer_body, out_shape=(jax.ShapeDtypeStruct((512, 1024), B...]
    ppermute x6 -> x3, starting transfers between devices: 7.14 us -> 7.96 us  [ahead(): lax.ppermute(value, 'page', [(s, (s + steps) % 64) for s in range(64)])]
  transfers between devices with their start and end apart: 8 -> 5, of which waited for: 4 -> 3; matrix products, arithmetic and copies ran while one was open for 3% -> 2% of each run, Pallas kernels for 38% -> 35%
where the time goes in v1:
time: 108 us
  Pallas kernels  49.6 us (46%)
  waiting for transfers between devices  42.4 us (39%)
  starting transfers between devices  11.3 us (10%)
  local copies, waits for them, and re-layouts  2.63 us (2%)
  other arithmetic  1.28 us (1%)
    pallas_call x1, Pallas kernels, layer(): pl.pallas_call(layer_body, out_shape=(jax.ShapeDtypeStruct((512, 1024), B...  29 us
    ppermute x2, waiting for transfers between devices, swap(): return lax.ppermute(value, 'head', [(0, 1), (1, 0)])  23.3 us
    ppermute x3, waiting for transfers between devices, ahead(): lax.ppermute(value, 'page', [(s, (s + steps) % 64) for s in range(64)])  19.1 us
    ppermute x3, starting transfers between devices, ahead(): lax.ppermute(value, 'page', [(s, (s + steps) % 64) for s in range(64)])  7.96 us
    pallas_call x1, Pallas kernels, fin(): pl.pallas_call(fin_body, out_shape=jax.ShapeDtypeStruct((16384, 128), B),...  7.07 us
    pallas_call x1, Pallas kernels, place(): pl.pallas_call(place_body, out_shape=jax.ShapeDtypeStruct((8, 256, 1024),...  4.95 us
    pallas_call x1, Pallas kernels, mix(): pl.pallas_call(mix_body, out_shape=jax.ShapeDtypeStruct((512, 1024), B),...  4.64 us
    pallas_call x1, Pallas kernels, pick(): pl.pallas_call(pick_body, out_shape=(jax.ShapeDtypeStruct((PAY, 1024), B)...  3.97 us
  transfers between devices with their start and end apart: 5, of which 3 were waited for; matrix products, arithmetic and copies ran while one was open for 2% of the time, Pallas kernels for 35%

profile of v1, /device:TPU:1, one launch (start us, length us, event | category | flops | bytes accessed | tf_op | source)
XLA Modules:
  0.0 107.9 jit_solution(12751232185932367343)
XLA Ops:
  0.6 4.6 %mix.1.own_ref = bf16[512,1024]{1,0:T(8,128)(2,1)} custom-call(f32[4]{0:T(128)} %r_ref.1, bf16[16384,128]{1,0:T(8,128)(2,1)} %bitcast.36), custom_call_target="tpu_custom_call" | custom-call | flops 100000000 | bytes 6291456 | tf_op jit(solution)/shard_map/mix/pallas_call | solution.py:172
  5.3 0.0 copy-start.2
  5.3 0.0 copy-start.3
  5.3 0.0 copy-start
  5.3 0.0 copy-start.4
  5.3 2.1 %collective-permute-start = (bf16[512,1024]{1,0:T(8,128)(2,1)}, bf16[512,1024]{1,0:T(8,128)(2,1)S(1)}, u32[]{:S(2)}, u32[]{:S(2)}) collective-permute-start(bf16[512,1024]{1,0:T(8,128)(2,1)} %mix.1.own_ref), channel_id=1, source_target_pairs={{0,64},{64,0},{1,65},{65,1},{2,66},{66,2},{3,67},{67,3},{4,68},{68... | collective-permute-start | bytes 3145736 | tf_op jit(solution)/shard_map/ppermute | solution.py:310
  7.4 4.0 %pick.1 = (bf16[528,1024]{1,0:T(8,128)(2,1)}, bf16[528,1024]{1,0:T(8,128)(2,1)}, bf16[528,1024]{1,0:T(8,128)(2,1)}) custom-call(s32[4]{0:T(128)} %tab.1, s32[1]{0:T(128)} %bitcast.9.me_ref, bf16[1024,1024]{1,0:T(8,128)(2,1)} %bitcast.38), custom_call_target="tpu_custom_call" | custom-call | bytes 6291456 | tf_op jit(solution)/shard_map/pick/pallas_call | solution.py:254
  11.4 2.2 %collective-permute-start.4 = (bf16[528,1024]{1,0:T(8,128)(2,1)}, bf16[528,1024]{1,0:T(8,128)(2,1)}, u32[]{:S(2)}, u32[]{:S(2)}) collective-permute-start(bf16[528,1024]{1,0:T(8,128)(2,1)} %get-tuple-element.21), channel_id=1, source_target_pairs={{0,3},{1,4},{2,5},{3,6},{4,7},{5,8},{6,9},{7,10},{8,11},{9,12},{10... | collective-permute-start | bytes 3244040 | tf_op jit(solution)/shard_map/ppermute | solution.py:307
  13.6 0.0 copy-done.2
  13.6 0.2 reduce-window.4
  13.8 0.0 copy-done.3
  13.8 0.1 select_reduce_fusion
  13.9 1.0 fusion
  14.9 15.2 %collective-permute-done.oth_ref = bf16[512,1024]{1,0:T(8,128)(2,1)S(1)} collective-permute-done((bf16[512,1024]{1,0:T(8,128)(2,1)}, bf16[512,1024]{1,0:T(8,128)(2,1)S(1)}, u32[]{:S(2)}, u32[]{:S(2)}) %collective-permute-start) | collective-permute-done | bytes 1048608 | tf_op jit(solution)/shard_map/ppermute | solution.py:310
  30.1 4.5 %collective-permute-start.2 = (bf16[528,1024]{1,0:T(8,128)(2,1)}, bf16[528,1024]{1,0:T(8,128)(2,1)}, u32[]{:S(2)}, u32[]{:S(2)}) collective-permute-start(bf16[528,1024]{1,0:T(8,128)(2,1)} %get-tuple-element.19), channel_id=1, source_target_pairs={{0,1},{1,2},{2,3},{3,4},{4,5},{5,6},{6,7},{7,8},{8,9},{9,10},{10,1... | collective-permute-start | bytes 3244040 | tf_op jit(solution)/shard_map/ppermute | solution.py:307
  34.7 1.2 %collective-permute-start.3 = (bf16[528,1024]{1,0:T(8,128)(2,1)}, bf16[528,1024]{1,0:T(8,128)(2,1)}, u32[]{:S(2)}, u32[]{:S(2)}) collective-permute-start(bf16[528,1024]{1,0:T(8,128)(2,1)} %get-tuple-element.20), channel_id=1, source_target_pairs={{0,2},{1,3},{2,4},{3,5},{4,6},{5,7},{6,8},{7,9},{8,10},{9,11},{10,... | collective-permute-start | bytes 3244040 | tf_op jit(solution)/shard_map/ppermute | solution.py:307
  35.9 0.0 copy-done
  35.9 0.0 copy-done.4
  35.9 0.0 copy-start.6
  35.9 29.0 %layer.1 = (bf16[512,1024]{1,0:T(8,128)(2,1)S(1)}, bf16[512,1024]{1,0:T(8,128)(2,1)}) custom-call(s32[4]{0:T(128)S(1)} %bitcast.33, s32[4]{0:T(128)S(1)} %bitcast.34, s32[12]{0:T(128)S(1)} %bitcast.35, s32[1]{0:T(128)} %bitcast.6.head_ref, bf16[512,1024]{1,0:T(8,128)(2,1)S(1)} %copy-done, bf16[512,1024]{1,0:T(8,128)(2,1)S(1)} %collective-permute-done.oth_ref, ...), custom_call_target="tpu_custom_call" | custom-call | flops 14000000000 | bytes 27262976 | tf_op jit(solution)/shard_map/layer/pallas_call | solution.py:123
  64.9 0.0 copy-start.1
  64.9 1.0 copy-done.1
  65.9 1.2 %collective-permute-start.1 = (bf16[512,1024]{1,0:T(8,128)(2,1)}, bf16[512,1024]{1,0:T(8,128)(2,1)S(1)}, u32[]{:S(2)}, u32[]{:S(2)}) collective-permute-start(bf16[512,1024]{1,0:T(8,128)(2,1)} %get-tuple-element.18), channel_id=1, source_target_pairs={{0,64},{64,0},{1,65},{65,1},{2,66},{66,2},{3,67},{67,3},{4,68},{68... | collective-permute-start | bytes 3145736 | tf_op jit(solution)/shard_map/ppermute | solution.py:310
  67.1 0.0 copy-done.6
  67.1 0.6 reshape.68.c_ref
  67.7 0.0 collective-permute-done.4.r3
  67.7 0.0 collective-permute-done.2.r1
  67.7 19.1 %collective-permute-done.3.r2 = bf16[528,1024]{1,0:T(8,128)(2,1)} collective-permute-done((bf16[528,1024]{1,0:T(8,128)(2,1)}, bf16[528,1024]{1,0:T(8,128)(2,1)}, u32[]{:S(2)}, u32[]{:S(2)}) %collective-permute-start.3) | collective-permute-done | bytes 1081376 | tf_op jit(solution)/shard_map/ppermute | solution.py:307
  86.8 5.0 %place.1 = bf16[8,256,1024]{2,1,0:T(8,128)(2,1)} custom-call(s32[4]{0:T(128)} %tab.1, s32[1]{0:T(128)} %bitcast.9.me_ref, bf16[1024,1024]{1,0:T(8,128)(2,1)} %bitcast.39, bf16[528,1024]{1,0:T(8,128)(2,1)} %collective-permute-done.2.r1, bf16[528,1024]{1,0:T(8,128)(2,1)} %collective-permute-done.3.r2, bf16[528,1024]{1,0:T(8,128)(2,1)} %collective-permute-done.4.r3), custom_call_target="tpu_custom_call" | custom-call | bytes 8388608 | tf_op jit(solution)/shard_map/place/pallas_call | solution.py:298
  91.8 8.1 %collective-permute-done.1.b_ref = bf16[512,1024]{1,0:T(8,128)(2,1)S(1)} collective-permute-done((bf16[512,1024]{1,0:T(8,128)(2,1)}, bf16[512,1024]{1,0:T(8,128)(2,1)S(1)}, u32[]{:S(2)}, u32[]{:S(2)}) %collective-permute-start.1) | collective-permute-done | bytes 1048608 | tf_op jit(solution)/shard_map/ppermute | solution.py:310
  99.9 1.0 copy-done.5
  100.9 7.1 %fin.1 = bf16[16384,128]{1,0:T(8,128)(2,1)} custom-call(f32[16]{0:T(128)} %reshape.68.c_ref, f32[4]{0:T(128)} %w_ref.1, bf16[16384,128]{1,0:T(8,128)(2,1)} %bitcast.37, bf16[512,1024]{1,0:T(8,128)(2,1)} %copy-done.1, bf16[512,1024]{1,0:T(8,128)(2,1)} %copy-done.5), custom_call_target="tpu_custom_call" | custom-call | flops 1000000000 | bytes 10485760 | tf_op jit(solution)/shard_map/fin/pallas_call | solution.py:218
  (5 shorter events, 0.0 us)
Async XLA Ops:
  5.3 8.3 %copy-start.2 = (s32[1,4]{1,0:T(1,128)S(1)}, s32[1,4]{1,0:T(1,128)}, u32[]{:S(2)}) copy-start(s32[1,4]{1,0:T(1,128)} %param.18) | copy-start | bytes 52
  5.3 8.5 %copy-start.3 = (s32[1,4]{1,0:T(1,128)S(1)}, s32[1,4]{1,0:T(1,128)}, u32[]{:S(2)}) copy-start(s32[1,4]{1,0:T(1,128)} %param.19) | copy-start | bytes 52
  5.3 30.6 %copy-start = (bf16[512,1024]{1,0:T(8,128)(2,1)S(1)}, bf16[512,1024]{1,0:T(8,128)(2,1)}, u32[]{:S(2)}) copy-start(bf16[512,1024]{1,0:T(8,128)(2,1)} %mix.1.own_ref) | copy-start | bytes 3145732
  5.3 30.6 %copy-start.4 = (s32[1,12]{1,0:T(1,128)S(1)}, s32[1,12]{1,0:T(1,128)}, u32[]{:S(2)}) copy-start(s32[1,12]{1,0:T(1,128)} %param.20) | copy-start | bytes 148
  5.3 24.8 %collective-permute-start = (bf16[512,1024]{1,0:T(8,128)(2,1)}, bf16[512,1024]{1,0:T(8,128)(2,1)S(1)}, u32[]{:S(2)}, u32[]{:S(2)}) collective-permute-start(bf16[512,1024]{1,0:T(8,128)(2,1)} %mix.1.own_ref), channel_id=1, source_target_pairs={{0,64},{64,0},{1,65},{65,1},{2,66},{66,2},{3,67},{67,3},{4,68},{68... | collective-permute-start | bytes 3145736 | tf_op jit(solution)/shard_map/ppermute | solution.py:310
  11.4 56.3 %collective-permute-start.4 = (bf16[528,1024]{1,0:T(8,128)(2,1)}, bf16[528,1024]{1,0:T(8,128)(2,1)}, u32[]{:S(2)}, u32[]{:S(2)}) collective-permute-start(bf16[528,1024]{1,0:T(8,128)(2,1)} %get-tuple-element.21), channel_id=1, source_target_pairs={{0,3},{1,4},{2,5},{3,6},{4,7},{5,8},{6,9},{7,10},{8,11},{9,12},{10... | collective-permute-start | bytes 3244040 | tf_op jit(solution)/shard_map/ppermute | solution.py:307
  30.1 37.6 %collective-permute-start.2 = (bf16[528,1024]{1,0:T(8,128)(2,1)}, bf16[528,1024]{1,0:T(8,128)(2,1)}, u32[]{:S(2)}, u32[]{:S(2)}) collective-permute-start(bf16[528,1024]{1,0:T(8,128)(2,1)} %get-tuple-element.19), channel_id=1, source_target_pairs={{0,1},{1,2},{2,3},{3,4},{4,5},{5,6},{6,7},{7,8},{8,9},{9,10},{10,1... | collective-permute-start | bytes 3244040 | tf_op jit(solution)/shard_map/ppermute | solution.py:307
  34.7 52.2 %collective-permute-start.3 = (bf16[528,1024]{1,0:T(8,128)(2,1)}, bf16[528,1024]{1,0:T(8,128)(2,1)}, u32[]{:S(2)}, u32[]{:S(2)}) collective-permute-start(bf16[528,1024]{1,0:T(8,128)(2,1)} %get-tuple-element.20), channel_id=1, source_target_pairs={{0,2},{1,3},{2,4},{3,5},{4,6},{5,7},{6,8},{7,9},{8,10},{9,11},{10,... | collective-permute-start | bytes 3244040 | tf_op jit(solution)/shard_map/ppermute | solution.py:307
  35.9 31.2 %copy-start.6 = (f32[4,4]{1,0:T(4,128)S(1)}, f32[4,4]{1,0:T(4,128)}, u32[]{:S(2)}) copy-start(f32[4,4]{1,0:T(4,128)} %param.14) | copy-start | bytes 196
  64.9 1.0 copy-start.1
  65.9 34.0 %collective-permute-start.1 = (bf16[512,1024]{1,0:T(8,128)(2,1)}, bf16[512,1024]{1,0:T(8,128)(2,1)S(1)}, u32[]{:S(2)}, u32[]{:S(2)}) collective-permute-start(bf16[512,1024]{1,0:T(8,128)(2,1)} %get-tuple-element.18), channel_id=1, source_target_pairs={{0,64},{64,0},{1,65},{65,1},{2,66},{66,2},{3,67},{67,3},{4,68},{68... | collective-permute-start | bytes 3145736 | tf_op jit(solution)/shard_map/ppermute | solution.py:310
  99.9 1.0 copy-start.5

commit v2 on v1

v2 whole, which is shorter than its diff:
```python
import functools
import math

import jax
import jax.numpy as jnp
from jax import lax
from jax.experimental import pallas as pl
from jax.experimental.pallas import tpu as pltpu
from jax.sharding import PartitionSpec as P

F=jnp.float32; B=jnp.bfloat16
NEG=-1e30
def io(shape,d): return lax.broadcasted_iota(jnp.int32,shape,d)
def dot_t(a,b): return lax.dot_general(a,b,(((1,),(1,)),((),())),preferred_element_type=F)
def dot(a,b): return jnp.dot(a,b,preferred_element_type=F)
QSCALE=math.log2(math.e)/math.sqrt(128.0)

def proj_body(head_ref,own0,own1,oth0,oth1,cos_ref,sin_ref,wq,wk,wv,q,k,v,nrm):
    h=head_ref[0]
    hoff=pl.multiple_of(h*1024,1024); ooff=pl.multiple_of((1-h)*1024,1024)
    for half,(own_ref,oth_ref) in enumerate(((own0,oth0),(own1,oth1))):
        def ln(i,_,half=half,own_ref=own_ref,oth_ref=oth_ref):
            r=pl.ds(pl.multiple_of(i*16,16),16)
            o=pl.ds(pl.multiple_of(half*256+i*16,16),16)
            a=own_ref[r,:].astype(F); b=oth_ref[r,:].astype(F)
            m=jnp.sum(a+b,axis=1,keepdims=True)*(1.0/2048)
            a=a-m; b=b-m
            var=jnp.sum(a*a+b*b,axis=1,keepdims=True)*(1.0/2048)
            rs=lax.rsqrt(var+1e-5)
            nrm[o,pl.ds(hoff,1024)]=(a*rs).astype(B)
            nrm[o,pl.ds(ooff,1024)]=(b*rs).astype(B)
            return 0
        lax.fori_loop(0,16,ln,0,unroll=8)
    for c,dst,w in ((0,q,wq),(1,k,wk),(2,v,wv)):
        def proj(i,_,c=c,dst=dst,w=w):
            col=pl.ds(pl.multiple_of(i*256,256),256)
            for rb in range(2):
                rows=slice(rb*256,rb*256+256)
                x=dot(nrm[rows,:],w[:,col])
                if c<2:
                    co=cos_ref[rows,:]; si=sin_ref[rows,:]
                    y=[]
                    for hh in range(2):
                        xh=x[:,hh*128:hh*128+128]
                        z=xh*co+pltpu.roll(xh,64,1)*si
                        if c==0: z=z*QSCALE
                        y.append(z)
                    x=jnp.concatenate(y,axis=1)
                dst[rows,col]=x.astype(B)
            return 0
        lax.fori_loop(0,4,proj,0)

def proj(head,own0,own1,oth0,oth1,cos,sin,wq,wk,wv):
    vm=pl.BlockSpec(memory_space=pltpu.VMEM); sm=pl.BlockSpec(memory_space=pltpu.SMEM)
    return pl.pallas_call(proj_body,out_shape=(jax.ShapeDtypeStruct((512,1024),B),)*3,
        in_specs=[sm]+[vm]*9,out_specs=(vm,)*3,scratch_shapes=[pltpu.VMEM((512,2048),B)],
        compiler_params=pltpu.CompilerParams(vmem_limit_bytes=12<<20),
        cost_estimate=pl.CostEstimate(flops=7*10**9,bytes_accessed=16<<20,transcendentals=0),
        name='proj')(head,own0,own1,oth0,oth1,cos,sin,wq,wk,wv)

def attn_body(len_ref,age_ref,head_ref,q,k,v,kc,vc,wo_hbm,*rest):
    keeps=rest[:NF]; sends=rest[NF:2*NF]
    (wo,att,s_ref,p_ref,acc,wosem)=rest[2*NF:]
    wocp=pltpu.make_async_copy(wo_hbm,wo,wosem)
    wocp.start()
    h=head_ref[0]
    hoff=pl.multiple_of(h*1024,1024); ooff=pl.multiple_of((1-h)*1024,1024)
    e=[len_ref[0],len_ref[0]+len_ref[1],len_ref[0]+len_ref[1]+len_ref[2]]
    def tile(t,_):
        t0=t*128
        rows=pl.ds(pl.multiple_of(t0,128),128)
        kb=jnp.maximum(t-2,0)*128
        win=pl.ds(pl.multiple_of(kb,128),384)
        ri=t0+io((128,384),0); ki=kb+io((128,384),1)
        st=jnp.where(ri>=e[2],e[2],jnp.where(ri>=e[1],e[1],jnp.where(ri>=e[0],e[0],0)))
        bias=jnp.where((ki>=st)&(ki<=ri),0.0,NEG)
        for hh in range(8):
            hs=slice(hh*128,hh*128+128)
            s_ref[hh,:,384:768]=dot_t(q[rows,hs],k[win,hs])+bias
        rid=t0+io((128,1),0)
        rreq=(rid>=e[0]).astype(jnp.int32)+(rid>=e[1]).astype(jnp.int32)+(rid>=e[2]).astype(jnp.int32)
        last=t0+127
        lo=(t0>=e[0]).astype(jnp.int32)+(t0>=e[1]).astype(jnp.int32)+(t0>=e[2]).astype(jnp.int32)
        hi=(last>=e[0]).astype(jnp.int32)+(last>=e[1]).astype(jnp.int32)+(last>=e[2]).astype(jnp.int32)
        def sc(r,_):
            cb=jnp.where(io((1,384),1)<age_ref[r],0.0,NEG)
            keys=pl.ds(pl.multiple_of(r*384,384),384)
            mine=rreq==r
            for hh in range(8):
                hs=slice(hh*128,hh*128+128)
                x=dot_t(q[rows,hs],kc[keys,hs])+cb
                s_ref[hh,:,0:384]=jnp.where(mine,x,s_ref[hh,:,0:384])
            return 0
        lax.fori_loop(lo,hi+1,sc,0)
        for hh in range(8):
            hs=slice(hh*128,hh*128+128)
            s=s_ref[hh]
            m=jnp.max(s,axis=1,keepdims=True)
            p=jnp.exp2(s-m)
            l=jnp.sum(p,axis=1,keepdims=True)
            p=(p*(1.0/l)).astype(B)
            p_ref[hh]=p[:,0:384]
            acc[:,hs]=dot(p[:,384:768],v[win,hs])
        def pv(r,_):
            keys=pl.ds(pl.multiple_of(r*384,384),384)
            mine=rreq==r
            for hh in range(8):
                hs=slice(hh*128,hh*128+128)
                pm=jnp.where(mine,p_ref[hh],jnp.zeros((),B))
                acc[:,hs]=acc[:,hs]+dot(pm,vc[keys,hs])
            return 0
        lax.fori_loop(lo,hi+1,pv,0)
        att[rows,:]=acc[...].astype(B)
        return 0
    lax.fori_loop(0,4,tile,0)
    wocp.wait()
    def outp(i,_):
        lc=pl.multiple_of(i*256,256)
        for rb in range(4):
            rows=slice(rb*128,rb*128+128)
            p=max(i for i in range(NF) if CUTS[i]<=rb*128)
            to=slice(rb*128-CUTS[p],rb*128-CUTS[p]+128)
            for dst,off in ((sends[p],ooff),(keeps[p],hoff)):
                dst[to,pl.ds(lc,256)]=dot(att[rows,:],wo[:,pl.ds(pl.multiple_of(off+lc,256),256)]).astype(B)
        return 0
    lax.fori_loop(0,4,outp,0)

def attn(lens,age,head,q,k,v,kc,vc,wo):
    vm=pl.BlockSpec(memory_space=pltpu.VMEM); an=pl.BlockSpec(memory_space=pl.ANY); sm=pl.BlockSpec(memory_space=pltpu.SMEM)
    return pl.pallas_call(attn_body,
        out_shape=tuple(jax.ShapeDtypeStruct((CUTS[i+1]-CUTS[i],1024),B) for i in range(NF))*2,
        in_specs=[sm]*3+[vm]*5+[an], out_specs=(vm,)*(2*NF),
        scratch_shapes=[pltpu.VMEM((1024,2048),B),pltpu.VMEM((512,1024),B),
            pltpu.VMEM((8,128,768),F),pltpu.VMEM((8,128,384),B),pltpu.VMEM((128,1024),F),pltpu.SemaphoreType.DMA],
        compiler_params=pltpu.CompilerParams(vmem_limit_bytes=40<<20),
        cost_estimate=pl.CostEstimate(flops=7*10**9,bytes_accessed=16<<20,transcendentals=4<<20),
        name='attn')(lens,age,head,q,k,v,kc,vc,wo)

def prep_body(order_ref,w_hbm,kv_hbm,wq,wk,wv,kc,vc,wsem,csem):
    cps=[pltpu.make_async_copy(w_hbm.at[c],w,wsem.at[c]) for c,w in enumerate((wq,wk,wv))]
    for i in range(12):
        pg=order_ref[i]
        cps.append(pltpu.make_async_copy(kv_hbm.at[pg,0],kc.at[pl.ds(i*128,128),:],csem.at[2*i]))
        cps.append(pltpu.make_async_copy(kv_hbm.at[pg,1],vc.at[pl.ds(i*128,128),:],csem.at[2*i+1]))
    for c in cps: c.start()
    for c in cps: c.wait()

def prep(order,w3,kv):
    vm=pl.BlockSpec(memory_space=pltpu.VMEM); an=pl.BlockSpec(memory_space=pl.ANY); sm=pl.BlockSpec(memory_space=pltpu.SMEM)
    return pl.pallas_call(prep_body,
        out_shape=tuple(jax.ShapeDtypeStruct(s,B) for s in ((2048,1024),)*3+((1536,1024),)*2),
        in_specs=[sm,an,an],out_specs=(vm,)*5,
        scratch_shapes=[pltpu.SemaphoreType.DMA((3,)),pltpu.SemaphoreType.DMA((24,))],
        compiler_params=pltpu.CompilerParams(vmem_limit_bytes=30<<20),
        cost_estimate=pl.CostEstimate(flops=0,bytes_accessed=46<<20,transcendentals=0),
        name='prep')(order,w3,kv)

def tables(lens,age):
    ends=jnp.cumsum(lens); starts=ends-lens
    t=jnp.arange(512,dtype=jnp.int32)
    mem=((t[:,None]>=starts[None,:])&(t[:,None]<ends[None,:])).astype(jnp.int32)
    pos=t+jnp.sum(mem*(age-starts)[None,:],axis=1)
    j=jnp.arange(128,dtype=jnp.int32)
    freq=10000.0**(-2.0*(j%64).astype(F)/128)
    ang=pos.astype(F)[:,None]*freq[None,:]
    return jnp.cos(ang), jnp.where(j[None,:]<64,-1.0,1.0)*jnp.sin(ang)

def rows_view(x):
    return x.reshape(512,4,8,128).transpose(0,2,1,3).reshape(16384,128)

def rows_unview(x):
    return x.reshape(512,8,4,128).transpose(0,2,1,3).reshape(512,4,1024)

MR=256
NCH=4
TCH=MR//NCH

def mix_body(base,r_ref,x_hbm,o_ref,x,sem):
    cps=[pltpu.make_async_copy(x_hbm.at[pl.ds(base*32+c*TCH*32,TCH*32),:],x.at[pl.ds(c*TCH*32,TCH*32),:],sem.at[c]) for c in range(NCH)]
    for c in cps: c.start()
    sh=(64,256); row=io(sh,0); col=io(sh,1)
    c=col&3
    a=jnp.where(c==0,r_ref[0],jnp.where(c==1,r_ref[1],jnp.where(c==2,r_ref[2],r_ref[3])))
    a=jnp.where(((col>>5)==(row&7))&(((col>>2)&7)==(row>>3)),a,0.0)
    hi=a.astype(B)
    A=jnp.concatenate([hi,(a-hi.astype(F)).astype(B)],axis=0)
    for ch in range(NCH):
        cps[ch].wait()
        for g in range(ch*TCH//16,(ch+1)*TCH//16):
            X=jnp.concatenate([x[g*512:g*512+256,:],x[g*512+256:g*512+512,:]],axis=1)
            o=dot(A,X)
            o=o[0:64]+o[64:128]
            for j in range(8):
                o_ref[g*16:g*16+16,j*128:(j+1)*128]=jnp.concatenate([o[j*8:j*8+8,0:128],o[j*8:j*8+8,128:256]],axis=0).astype(B)

def mix(i,x,r):
    return pl.pallas_call(functools.partial(mix_body,i*MR),out_shape=jax.ShapeDtypeStruct((MR,1024),B),
      in_specs=[pl.BlockSpec(memory_space=pltpu.SMEM),pl.BlockSpec(memory_space=pl.ANY)],
      out_specs=pl.BlockSpec(memory_space=pltpu.VMEM),
      scratch_shapes=[pltpu.VMEM((MR*32,128),B),pltpu.SemaphoreType.DMA((NCH,))],
      compiler_params=pltpu.CompilerParams(vmem_limit_bytes=61<<20),
      cost_estimate=pl.CostEstimate(flops=10**8,bytes_accessed=3<<20,transcendentals=0),
      name='mix')(r,x)

CUTS=(0,384,512)
NF=2
STEP=64

def fin_body(base,size,c_ref,w_ref,x_hbm,a_ref,b_ref,*rest):
    o_hbm,x,o,m_ref,wm_ref,isem,osem=rest[-7:]
    FCH=size//STEP
    def span(c): return pl.ds((base+c*STEP)*32,STEP*32)
    def part(c): return pl.ds(c*STEP*32,STEP*32)
    icp=[pltpu.make_async_copy(x_hbm.at[span(c),:],x.at[part(c),:],isem.at[c]) for c in range(FCH)]
    ocp=[pltpu.make_async_copy(o.at[part(c),:],o_hbm.at[span(c),:],osem.at[c]) for c in range(FCH)]
    for c in icp: c.start()
    n=128
    row=io((n,n),0); col=io((n,n),1)
    a=jnp.zeros((n,n),F)
    for i in range(4):
        for j in range(4):
            a=jnp.where(((row&3)==j)&((col&3)==i),c_ref[i*4+j],a)
    a=jnp.where((row>>2)==(col>>2),a,0.0)
    hi=a.astype(B); m_ref[:,0:n]=hi; m_ref[:,n:2*n]=(a-hi.astype(F)).astype(B)
    for s in range(2):
        row=io((n,64),0); col=io((n,64),1)
        a=jnp.zeros((n,64),F)
        for j in range(4): a=jnp.where((row&3)==j,w_ref[j],a)
        a=jnp.where(((row>>5)+s*4==(col&7))&(((row>>2)&7)==(col>>3)),a,0.0)
        hi=a.astype(B); lo=(a-hi.astype(F)).astype(B)
        wm_ref[s*n:(s+1)*n,:]=jnp.concatenate([hi,lo,hi,lo],axis=1)
    M=m_ref[...]
    for ch in range(FCH):
        icp[ch].wait()
        for g in range(ch*STEP//16,(ch+1)*STEP//16):
            def U(ref):
                u=ref[g*16:g*16+16,:].astype(F)
                return jnp.concatenate([jnp.concatenate([u[0:8,j*128:(j+1)*128],u[8:16,j*128:(j+1)*128]],axis=1) for j in range(8)],axis=0).astype(B)
            Ua=U(a_ref);Ub=U(b_ref)
            ou=dot(wm_ref[...],jnp.concatenate([Ua,Ua,Ub,Ub],axis=0))
            r0=g*512
            for s in range(2):
                X=jnp.concatenate([x[r0+s*128:r0+s*128+128,:],x[r0+256+s*128:r0+256+s*128+128,:]],axis=1)
                z=(dot(M,jnp.concatenate([X,X],axis=0))+ou[s*128:(s+1)*128]).astype(B)
                o[r0+s*128:r0+s*128+128,:]=z[:,0:128]; o[r0+256+s*128:r0+256+s*128+128,:]=z[:,128:256]
        ocp[ch].start()
    for c in ocp: c.wait()

def fin(i,x,u1,u2,cr,w,prev):
    an=pl.BlockSpec(memory_space=pl.ANY); sm=pl.BlockSpec(memory_space=pltpu.SMEM); vm=pl.BlockSpec(memory_space=pltpu.VMEM)
    more=[] if prev is None else [prev]
    base,size=CUTS[i],CUTS[i+1]-CUTS[i]
    return pl.pallas_call(functools.partial(fin_body,base,size),out_shape=jax.ShapeDtypeStruct((16384,128),B),
      in_specs=[sm,sm,an,vm,vm]+[an]*len(more),out_specs=an,
      scratch_shapes=[pltpu.VMEM((size*32,128),B),pltpu.VMEM((size*32,128),B),pltpu.VMEM((128,256),B),pltpu.VMEM((256,256),B),
        pltpu.SemaphoreType.DMA((size//STEP,)),pltpu.SemaphoreType.DMA((size//STEP,))],
      input_output_aliases={5:0} if more else {},
      compiler_params=pltpu.CompilerParams(vmem_limit_bytes=58<<20),
      cost_estimate=pl.CostEstimate(flops=10**9*size//512,bytes_accessed=(10<<20)*size//512,transcendentals=0),
      name='fin')(cr,w,x,u1,u2,*more)

ROWS=2048
PAY=2*ROWS+16

def tiles_view(x):
    n=x.shape[0]
    return x.reshape(n//8,8,8,128).transpose(0,2,1,3).reshape(n*8,128)

def tiles_unview(x):
    n=x.shape[0]//8
    return x.reshape(n//8,8,8,128).transpose(0,2,1,3).reshape(n,1024)

def pick_body(tab_ref,me_ref,src,o1,o2,o3,buf,lab,isem,osem):
    me=me_ref[0]
    icp=[pltpu.make_async_copy(src.at[pl.ds(b*ROWS,ROWS),:],buf.at[b],isem.at[b]) for b in range(4)]
    for c in icp: c.start()
    plan=[]
    for d,dst in ((3,o3),(2,o2),(1,o1)):
        cnt=jnp.int32(0); i=[jnp.int32(0)]*2; l=[jnp.int32(-1)]*2
        for b in range(4):
            hit=(((tab_ref[b]>>3)-me)&63)==d
            for s in range(2):
                i[s]=jnp.where(hit&(cnt==s),b,i[s])
                l[s]=jnp.where(hit&(cnt==s),tab_ref[b]&7,l[s])
            cnt=cnt+hit.astype(jnp.int32)
        lab[d-1]=jnp.where(io((16,128),0)<8,l[0].astype(F),l[1].astype(F)).astype(B)
        plan.append((d,dst,i))
    for c in icp: c.wait()
    cps=[]
    for d,dst,i in plan:
        for s in range(2):
            cps.append(pltpu.make_async_copy(buf.at[i[s]],dst.at[pl.ds(s*ROWS,ROWS),:],osem.at[3*(d-1)+s]))
        cps.append(pltpu.make_async_copy(lab.at[d-1],dst.at[pl.ds(2*ROWS,16),:],osem.at[3*(d-1)+2]))
    for c in cps: c.start()
    for c in cps: c.wait()

def pick(tab,me,pre):
    an=pl.BlockSpec(memory_space=pl.ANY); sm=pl.BlockSpec(memory_space=pltpu.SMEM)
    return pl.pallas_call(pick_body,out_shape=(jax.ShapeDtypeStruct((PAY,128),B),)*3,
      in_specs=[sm,sm,an],out_specs=(an,)*3,
      scratch_shapes=[pltpu.VMEM((4,ROWS,128),B),pltpu.VMEM((3,16,128),B),pltpu.SemaphoreType.DMA((4,)),pltpu.SemaphoreType.DMA((9,))],
      compiler_params=pltpu.CompilerParams(vmem_limit_bytes=12<<20),
      cost_estimate=pl.CostEstimate(flops=0,bytes_accessed=6<<20,transcendentals=0),
      name='pick')(tab,me,pre)

def place_body(tab,me_ref,src,r1,r3,r2,out,buf,zero,isem,osem):
    me=me_ref[0]
    used=jnp.int32(0)
    for b in range(4):
        hit=(tab[b]>>3)==me
        slot=tab[b]&7
        @pl.when(hit)
        def _(b=b,slot=slot):
            pltpu.make_async_copy(src.at[pl.ds(b*ROWS,ROWS),:],buf.at[slot],isem.at[slot]).start()
        used=used|jnp.where(hit,jnp.int32(1)<<slot,0)
    here=used
    for ref,on in ((r1,True),(r3,True),(r2,True)):
        lab=ref[2*ROWS:2*ROWS+16,:].astype(F)
        for s in range(2):
            v=jnp.max(lab[s*8:s*8+8]).astype(jnp.int32)
            hit=(v>=0)&on
            slot=v&7
            @pl.when(hit)
            def _(ref=ref,s=s,slot=slot):
                pltpu.make_async_copy(ref.at[pl.ds(s*ROWS,ROWS),:],out.at[slot],osem.at[slot]).start()
            used=used|jnp.where(hit,jnp.int32(1)<<slot,0)
    zero[...]=jnp.zeros_like(zero)
    for s in range(8):
        @pl.when(((used>>s)&1)==0)
        def _(s=s):
            pltpu.make_async_copy(zero,out.at[s],osem.at[s]).start()
    for s in range(8):
        @pl.when(((here>>s)&1)==1)
        def _(s=s):
            pltpu.make_async_copy(src.at[pl.ds(0,ROWS),:],buf.at[s],isem.at[s]).wait()
            pltpu.make_async_copy(buf.at[s],out.at[s],osem.at[s]).start()
    for s in range(8):
        pltpu.make_async_copy(zero,out.at[s],osem.at[s]).wait()

def place(tab,me,pre,*got):
    an=pl.BlockSpec(memory_space=pl.ANY); sm=pl.BlockSpec(memory_space=pltpu.SMEM); vm=pl.BlockSpec(memory_space=pltpu.VMEM)
    return pl.pallas_call(place_body,out_shape=jax.ShapeDtypeStruct((8,ROWS,128),B),
      in_specs=[sm,sm,an,vm,vm,vm],out_specs=an,
      scratch_shapes=[pltpu.VMEM((8,ROWS,128),B),pltpu.VMEM((ROWS,128),B),
        pltpu.SemaphoreType.DMA((8,)),pltpu.SemaphoreType.DMA((8,))],
      compiler_params=pltpu.CompilerParams(vmem_limit_bytes=12<<20),
      cost_estimate=pl.CostEstimate(flops=0,bytes_accessed=8<<20,transcendentals=0),
      name='place')(tab,me,pre,*got)

def ahead(value,steps):
    return lax.ppermute(value,"page",[(s,(s+steps)%64) for s in range(64)])

def swap(value):
    return lax.ppermute(value,"head",[(0,1),(1,0)])

def body(streams,hc_read,hc_carry,hc_write,w_qkv,w_out,req_lengths,req_age,cache_order,cache_kv,prefill_kv,page_table):
    head=lax.axis_index("head").astype(jnp.int32).reshape(1)
    me=lax.axis_index("page").astype(jnp.int32).reshape(1)
    lens=req_lengths[0]; age=req_age[0]; order=cache_order[0]
    x=rows_view(streams)
    own0=mix(0,x,hc_read)
    oth0=swap(own0)
    x1,own0=lax.optimization_barrier((x,own0))
    own1=mix(1,x1,hc_read)
    oth1=swap(own1)
    pre=tiles_view(prefill_kv.reshape(1024,1024))
    own_dep,table=lax.optimization_barrier((own1,page_table))
    s1,s2,s3=pick(table,me,pre)
    r3=ahead(s3,3); r1=ahead(s1,1)
    cos,sin=tables(lens,age)
    wq,wk,wv,kc,vc=prep(order,w_qkv.transpose(1,0,2),cache_kv)
    oth1,s2,wq,wk,wv,kc,vc=lax.optimization_barrier((oth1,s2,wq,wk,wv,kc,vc))
    r2=ahead(s2,2)
    q,k,v=proj(head,own0,own1,oth0,oth1,cos,sin,wq,wk,wv)
    parts=attn(lens,age,head,q,k,v,kc,vc,w_out)
    keeps,sends=parts[:NF],parts[NF:]
    recvs=[swap(s) for s in sends]
    pages=place(page_table,me,pre,r1,r3,r2)
    carry=(jnp.eye(4,dtype=F)+hc_carry).reshape(16)
    recvs[0],pages=lax.optimization_barrier((recvs[0],pages))
    new=None
    for i in range(NF): new=fin(i,x,keeps[i],recvs[i],carry,hc_write,new)
    return rows_unview(new),tiles_unview(pages.reshape(8*ROWS,128)).reshape(8,1,2,128,1024)

def solution(mesh):
    placed=(P("page",None,"head"),P(),P(),P(),P(None,None,"head"),P("head",None),P("page",None),P("page",None),P("page",None),
        P("page",None,None,"head"),P("page",None,None,None,"head"),P("page"))
    return jax.shard_map(body,mesh=mesh,in_specs=placed,out_specs=(P("page",None,"head"),P("page",None,None,None,"head")),check_vma=False)
```

time: 108 us -> 103 us (0.954); the launches traced: 108 us -> 101 us
  waiting for transfers between devices: 42.4 us -> 27.7 us
  Pallas kernels: 49.6 us -> 57.8 us
    ppermute x2 -> x4, waiting for transfers between devices: 23.3 us -> 7.86 us  [swap(): return lax.ppermute(value, 'head', [(0, 1), (1, 0)])]
    pallas_call x5 -> x9, Pallas kernels: 49.6 us -> 57.8 us  [the longest x1 14.7 us: attn(): pl.pallas_call(attn_body, out_shape=tuple((jax.ShapeDtypeStruct((CUTS[i +...]
    ppermute x2 -> x4, starting transfers between devices: 3.32 us -> 3.68 us  [swap(): return lax.ppermute(value, 'head', [(0, 1), (1, 0)])]
  transfers between devices with their start and end apart: 5 -> 7, of which waited for: 3 -> 3; matrix products, arithmetic and copies ran while one was open for 2% -> 2% of each run, Pallas kernels for 35% -> 50%
where the time goes in v2:
time: 103 us; the launch traced here: 101 us
  Pallas kernels  57.8 us (56%)
  waiting for transfers between devices  27.7 us (27%)
  starting transfers between devices  11 us (11%)
  local copies, waits for them, and re-layouts  2.28 us (2%)
  other arithmetic  1.28 us (1%)
    ppermute x3, waiting for transfers between devices, ahead(): lax.ppermute(value, 'page', [(s, (s + steps) % 64) for s in range(64)])  19.9 us
    pallas_call x1, Pallas kernels, attn(): pl.pallas_call(attn_body, out_shape=tuple((jax.ShapeDtypeStruct((CUTS[i +...  14.7 us
    pallas_call x1, Pallas kernels, proj(): pl.pallas_call(proj_body, out_shape=(jax.ShapeDtypeStruct((512, 1024), B)...  12.1 us
    pallas_call x2, Pallas kernels, fin(): pl.pallas_call(functools.partial(fin_body, base, size), out_shape=jax.Sha...  9.78 us
    ppermute x4, waiting for transfers between devices, swap(): return lax.ppermute(value, 'head', [(0, 1), (1, 0)])  7.86 us
    ppermute x3, starting transfers between devices, ahead(): lax.ppermute(value, 'page', [(s, (s + steps) % 64) for s in range(64)])  7.34 us
    pallas_call x1, Pallas kernels, prep(): pl.pallas_call(prep_body, out_shape=tuple((jax.ShapeDtypeStruct(s, B) for...  7.16 us
    pallas_call x2, Pallas kernels, mix(): pl.pallas_call(functools.partial(mix_body, i * MR), out_shape=jax.ShapeDt...  7.11 us
  transfers between devices with their start and end apart: 7, of which 3 were waited for; matrix products, arithmetic and copies ran while one was open for 2% of the time, Pallas kernels for 50%

profile of v2, /device:TPU:1, one launch (start us, length us, event | category | flops | bytes accessed | tf_op | source)
XLA Modules:
  0.0 101.1 jit_solution(2062774446441931218)
XLA Ops:
  0.6 3.6 %mix.2.own0 = bf16[256,1024]{1,0:T(8,128)(2,1)} custom-call(f32[4]{0:T(128)} %r_ref.3, bf16[16384,128]{1,0:T(8,128)(2,1)} %bitcast.44), custom_call_target="tpu_custom_call" | custom-call | flops 100000000 | bytes 3145728 | tf_op jit(solution)/shard_map/mix/pallas_call | solution.py:197
  4.3 0.0 copy-start.7
  4.3 0.0 copy-start.8
  4.3 0.0 copy-start.6
  4.3 2.1 %collective-permute-start = (bf16[256,1024]{1,0:T(8,128)(2,1)}, bf16[256,1024]{1,0:T(8,128)(2,1)S(1)}, u32[]{:S(2)}, u32[]{:S(2)}) collective-permute-start(bf16[256,1024]{1,0:T(8,128)(2,1)} %mix.2.own0), channel_id=1, source_target_pairs={{0,64},{64,0},{1,65},{65,1},{2,66},{66,2},{3,67},{67,3},{4,68},{68... | collective-permute-start | bytes 1572872 | tf_op jit(solution)/shard_map/ppermute | solution.py:354
  6.4 3.5 %mix.3.own1 = bf16[256,1024]{1,0:T(8,128)(2,1)} custom-call(f32[4]{0:T(128)} %r_ref.3, bf16[16384,128]{1,0:T(8,128)(2,1)} %bitcast.45), custom_call_target="tpu_custom_call" | custom-call | flops 100000000 | bytes 3145728 | tf_op jit(solution)/shard_map/mix/pallas_call | solution.py:197
  9.9 0.1 collective-permute-start.1
  10.0 2.5 %pick.1 = (bf16[4112,128]{1,0:T(8,128)(2,1)}, bf16[4112,128]{1,0:T(8,128)(2,1)}, bf16[4112,128]{1,0:T(8,128)(2,1)}) custom-call(s32[4]{0:T(128)S(1)} %copy-done.5, s32[1]{0:T(128)} %bitcast.8.me_ref, bf16[8192,128]{1,0:T(8,128)(2,1)S(1)} %bitcast.38), custom_call_target="tpu_custom_call" | custom-call | bytes 6291456 | tf_op jit(solution)/shard_map/pick/pallas_call | solution.py:299
  12.6 4.2 %collective-permute-start.4 = (bf16[4112,128]{1,0:T(8,128)(2,1)}, bf16[4112,128]{1,0:T(8,128)(2,1)}, u32[]{:S(2)}, u32[]{:S(2)}) collective-permute-start(bf16[4112,128]{1,0:T(8,128)(2,1)} %get-tuple-element.51), channel_id=1, source_target_pairs={{0,1},{1,2},{2,3},{3,4},{4,5},{5,6},{6,7},{7,8},{8,9},{9,10},{10,1... | collective-permute-start | bytes 3158024 | tf_op jit(solution)/shard_map/ppermute | solution.py:351
  16.7 0.0 collective-permute-start.5
  16.7 0.2 reduce-window.4
  16.9 7.2 %prep.1 = (bf16[2048,1024]{1,0:T(8,128)(2,1)S(1)}, bf16[2048,1024]{1,0:T(8,128)(2,1)S(1)}, bf16[2048,1024]{1,0:T(8,128)(2,1)S(1)}, bf16[1536,1024]{1,0:T(8,128)(2,1)S(1)}, bf16[1536,1024]{1,0:T(8,128)(2,1)S(1)}) custom-call(s32[12]{0:T(128)S(1)} %bitcast.40, bf16[3,2048,1024]{2,1,0:T(8,128)(2,1)} %bitcast.49, bf16[12,2,128,1024]{3,2,1,0:T(8,128)(2,1)} %kv_hbm.1), custom_call_target="tpu_custom_call" | custom-call | bytes 48234496 | tf_op jit(solution)/shard_map/prep/pallas_call | solution.py:150
  24.1 0.1 select_reduce_fusion
  24.2 1.0 fusion
  25.2 3.9 %collective-permute-done.1.oth1 = bf16[256,1024]{1,0:T(8,128)(2,1)} collective-permute-done((bf16[256,1024]{1,0:T(8,128)(2,1)}, bf16[256,1024]{1,0:T(8,128)(2,1)}, u32[]{:S(2)}, u32[]{:S(2)}) %collective-permute-start.1) | collective-permute-done | bytes 524320 | tf_op jit(solution)/shard_map/ppermute | solution.py:354
  29.1 3.2 %collective-permute-start.6 = (bf16[4112,128]{1,0:T(8,128)(2,1)}, bf16[4112,128]{1,0:T(8,128)(2,1)}, u32[]{:S(2)}, u32[]{:S(2)}) collective-permute-start(bf16[4112,128]{1,0:T(8,128)(2,1)} %get-tuple-element.53), channel_id=1, source_target_pairs={{0,2},{1,3},{2,4},{3,5},{4,6},{5,7},{6,8},{7,9},{8,10},{9,11},{10,... | collective-permute-start | bytes 3158024 | tf_op jit(solution)/shard_map/ppermute | solution.py:351
  32.3 0.0 collective-permute-done.oth0
  32.3 12.1 %proj.1 = (bf16[512,1024]{1,0:T(8,128)(2,1)S(1)}, bf16[512,1024]{1,0:T(8,128)(2,1)S(1)}, bf16[512,1024]{1,0:T(8,128)(2,1)S(1)}) custom-call(s32[1]{0:T(128)} %bitcast.5.head_ref, bf16[256,1024]{1,0:T(8,128)(2,1)S(1)} %copy-done.2, bf16[256,1024]{1,0:T(8,128)(2,1)S(1)} %copy-done.3, bf16[256,1024]{1,0:T(8,128)(2,1)S(1)} %collective-permute-done.oth0, ...), custom_call_target="tpu_custom_call" | custom-call | flops 7000000000 | bytes 16777216 | tf_op jit(solution)/shard_map/proj/pallas_call | solution.py:55
  44.5 0.0 copy-start.9
  44.5 14.7 %attn.1 = (bf16[384,1024]{1,0:T(8,128)(2,1)S(1)}, bf16[128,1024]{1,0:T(8,128)(2,1)S(1)}, bf16[384,1024]{1,0:T(8,128)(2,1)S(1)}, bf16[128,1024]{1,0:T(8,128)(2,1)S(1)}) custom-call(s32[4]{0:T(128)S(1)} %bitcast.42, s32[4]{0:T(128)S(1)} %bitcast.43, s32[1]{0:T(128)} %bitcast.5.head_ref, bf16[512,1024]{1,0:T(8,128)(2,1)S(1)} %get-tuple-element.42.q, ...), custom_call_target="tpu_custom_call" | custom-call | flops 7000000000 | bytes 16777216 | tf_op jit(solution)/shard_map/attn/pallas_call | solution.py:130
  59.2 0.9 copy-done.1
  60.1 0.7 copy-done.4
  60.8 0.3 collective-permute-start.3
  61.1 1.2 %collective-permute-start.2 = (bf16[128,1024]{1,0:T(8,128)(2,1)S(1)}, bf16[128,1024]{1,0:T(8,128)(2,1)}, u32[]{:S(2)}, u32[]{:S(2)}) collective-permute-start(bf16[128,1024]{1,0:T(8,128)(2,1)S(1)} %get-tuple-element.48), channel_id=1, source_target_pairs={{0,64},{64,0},{1,65},{65,1},{2,66},{66,2},{3,67},{67,3},{4,68},{68... | collective-permute-start | bytes 786440 | tf_op jit(solution)/shard_map/ppermute | solution.py:354
  62.3 0.7 reshape.65.c_ref
  62.9 0.0 collective-permute-done.4.r1
  63.0 0.0 collective-permute-done.5.r3
  63.0 19.9 %collective-permute-done.6.r2 = bf16[4112,128]{1,0:T(8,128)(2,1)} collective-permute-done((bf16[4112,128]{1,0:T(8,128)(2,1)}, bf16[4112,128]{1,0:T(8,128)(2,1)}, u32[]{:S(2)}, u32[]{:S(2)}) %collective-permute-start.6) | collective-permute-done | bytes 1052704 | tf_op jit(solution)/shard_map/ppermute | solution.py:351
  82.8 4.4 %place.1 = bf16[8,2048,128]{2,1,0:T(8,128)(2,1)} custom-call(s32[4]{0:T(128)S(1)} %copy-done.5, s32[1]{0:T(128)} %bitcast.8.me_ref, bf16[8192,128]{1,0:T(8,128)(2,1)S(1)} %bitcast.39, bf16[4112,128]{1,0:T(8,128)(2,1)} %collective-permute-done.4.r1, bf16[4112,128]{1,0:T(8,128)(2,1)} %collective-permute-done.5.r3, bf16[4112,128]{1,0:T(8,128)(2,1)} %collective-permute-done.6.r2), custom_call_target="tpu_custom_call" | custom-call | bytes 8388608 | tf_op jit(solution)/shard_map/place/pallas_call | solution.py:342
  87.2 3.9 %collective-permute-done.3.b_ref = bf16[384,1024]{1,0:T(8,128)(2,1)} collective-permute-done((bf16[384,1024]{1,0:T(8,128)(2,1)S(1)}, bf16[384,1024]{1,0:T(8,128)(2,1)}, u32[]{:S(2)}, u32[]{:S(2)}) %collective-permute-start.3) | collective-permute-done | bytes 786464 | tf_op jit(solution)/shard_map/ppermute | solution.py:354
  91.1 6.0 %fin.2.rest_0_ = bf16[16384,128]{1,0:T(8,128)(2,1)} custom-call(f32[16]{0:T(128)} %reshape.65.c_ref, f32[4]{0:T(128)} %w_ref.3, bf16[16384,128]{1,0:T(8,128)(2,1)} %bitcast.46, bf16[384,1024]{1,0:T(8,128)(2,1)} %copy-done.1, bf16[384,1024]{1,0:T(8,128)(2,1)} %collective-permute-done.3.b_ref), custom_call_target="tpu_custom_call" | custom-call | flops 750000000 | bytes 7864320 | tf_op jit(solution)/shard_map/fin/pallas_call | solution.py:253
  97.1 3.8 %fin.3 = bf16[16384,128]{1,0:T(8,128)(2,1)} custom-call(f32[16]{0:T(128)} %reshape.65.c_ref, f32[4]{0:T(128)} %w_ref.3, bf16[16384,128]{1,0:T(8,128)(2,1)} %bitcast.47, bf16[128,1024]{1,0:T(8,128)(2,1)} %copy-done.4, bf16[128,1024]{1,0:T(8,128)(2,1)} %collective-permute-done.2.b_ref, bf16[16384,128]{1,0:T(8,128)(2,1)} %fin.2.rest_0_), custom_call_target="tpu_custom_call", output_to_operand_aliasing={{}: (5, {})} | custom-call | flops 250000000 | bytes 2621440 | tf_op jit(solution)/shard_map/fin/pallas_call | solution.py:253
  (19 shorter events, 0.1 us)
Async XLA Ops:
  0.6 9.4 %copy-start = (bf16[4,1,2,128,1024]{4,3,2,1,0:T(8,128)(2,1)S(1)}, bf16[4,1,2,128,1024]{4,3,2,1,0:T(8,128)(2,1)}, u32[]{:S(2)}) copy-start(bf16[4,1,2,128,1024]{4,3,2,1,0:T(8,128)(2,1)} %param.22) | copy-start | bytes 6291460
  0.6 9.4 %copy-start.5 = (s32[4]{0:T(128)S(1)}, s32[4]{0:T(128)}, u32[]{:S(2)}) copy-start(s32[4]{0:T(128)} %tab.1) | copy-start | bytes 52
  4.3 12.4 %copy-start.7 = (s32[1,4]{1,0:T(1,128)S(1)}, s32[1,4]{1,0:T(1,128)}, u32[]{:S(2)}) copy-start(s32[1,4]{1,0:T(1,128)} %param.18) | copy-start | bytes 52
  4.3 12.6 %copy-start.8 = (s32[1,4]{1,0:T(1,128)S(1)}, s32[1,4]{1,0:T(1,128)}, u32[]{:S(2)}) copy-start(s32[1,4]{1,0:T(1,128)} %param.19) | copy-start | bytes 52
  4.3 12.6 %copy-start.6 = (s32[1,12]{1,0:T(1,128)S(1)}, s32[1,12]{1,0:T(1,128)}, u32[]{:S(2)}) copy-start(s32[1,12]{1,0:T(1,128)} %param.20) | copy-start | bytes 148
  4.3 28.0 %collective-permute-start = (bf16[256,1024]{1,0:T(8,128)(2,1)}, bf16[256,1024]{1,0:T(8,128)(2,1)S(1)}, u32[]{:S(2)}, u32[]{:S(2)}) collective-permute-start(bf16[256,1024]{1,0:T(8,128)(2,1)} %mix.2.own0), channel_id=1, source_target_pairs={{0,64},{64,0},{1,65},{65,1},{2,66},{66,2},{3,67},{67,3},{4,68},{68... | collective-permute-start | bytes 1572872 | tf_op jit(solution)/shard_map/ppermute | solution.py:354
  9.9 19.2 %collective-permute-start.1 = (bf16[256,1024]{1,0:T(8,128)(2,1)}, bf16[256,1024]{1,0:T(8,128)(2,1)}, u32[]{:S(2)}, u32[]{:S(2)}) collective-permute-start(bf16[256,1024]{1,0:T(8,128)(2,1)} %mix.3.own1), channel_id=1, source_target_pairs={{0,64},{64,0},{1,65},{65,1},{2,66},{66,2},{3,67},{67,3},{4,68},{68... | collective-permute-start | bytes 1572872 | tf_op jit(solution)/shard_map/ppermute | solution.py:354
  12.6 50.4 %collective-permute-start.4 = (bf16[4112,128]{1,0:T(8,128)(2,1)}, bf16[4112,128]{1,0:T(8,128)(2,1)}, u32[]{:S(2)}, u32[]{:S(2)}) collective-permute-start(bf16[4112,128]{1,0:T(8,128)(2,1)} %get-tuple-element.51), channel_id=1, source_target_pairs={{0,1},{1,2},{2,3},{3,4},{4,5},{5,6},{6,7},{7,8},{8,9},{9,10},{10,1... | collective-permute-start | bytes 3158024 | tf_op jit(solution)/shard_map/ppermute | solution.py:351
  16.7 46.2 %collective-permute-start.5 = (bf16[4112,128]{1,0:T(8,128)(2,1)}, bf16[4112,128]{1,0:T(8,128)(2,1)}, u32[]{:S(2)}, u32[]{:S(2)}) collective-permute-start(bf16[4112,128]{1,0:T(8,128)(2,1)} %get-tuple-element.52), channel_id=1, source_target_pairs={{0,3},{1,4},{2,5},{3,6},{4,7},{5,8},{6,9},{7,10},{8,11},{9,12},{10... | collective-permute-start | bytes 3158024 | tf_op jit(solution)/shard_map/ppermute | solution.py:351
  16.9 15.4 %copy-start.2 = (bf16[256,1024]{1,0:T(8,128)(2,1)S(1)}, bf16[256,1024]{1,0:T(8,128)(2,1)}, u32[]{:S(2)}) copy-start(bf16[256,1024]{1,0:T(8,128)(2,1)} %mix.2.own0) | copy-start | bytes 1572868
  16.9 15.4 %copy-start.3 = (bf16[256,1024]{1,0:T(8,128)(2,1)S(1)}, bf16[256,1024]{1,0:T(8,128)(2,1)}, u32[]{:S(2)}) copy-start(bf16[256,1024]{1,0:T(8,128)(2,1)} %mix.3.own1) | copy-start | bytes 1572868
  29.1 53.7 %collective-permute-start.6 = (bf16[4112,128]{1,0:T(8,128)(2,1)}, bf16[4112,128]{1,0:T(8,128)(2,1)}, u32[]{:S(2)}, u32[]{:S(2)}) collective-permute-start(bf16[4112,128]{1,0:T(8,128)(2,1)} %get-tuple-element.53), channel_id=1, source_target_pairs={{0,2},{1,3},{2,4},{3,5},{4,6},{5,7},{6,8},{7,9},{8,10},{9,11},{10,... | collective-permute-start | bytes 3158024 | tf_op jit(solution)/shard_map/ppermute | solution.py:351
  44.5 17.8 %copy-start.9 = (f32[4,4]{1,0:T(4,128)S(1)}, f32[4,4]{1,0:T(4,128)}, u32[]{:S(2)}) copy-start(f32[4,4]{1,0:T(4,128)} %param.14) | copy-start | bytes 196
  59.2 0.9 copy-start.1
  60.1 0.7 copy-start.4
  60.8 30.3 %collective-permute-start.3 = (bf16[384,1024]{1,0:T(8,128)(2,1)S(1)}, bf16[384,1024]{1,0:T(8,128)(2,1)}, u32[]{:S(2)}, u32[]{:S(2)}) collective-permute-start(bf16[384,1024]{1,0:T(8,128)(2,1)S(1)} %get-tuple-element.50), channel_id=1, source_target_pairs={{0,64},{64,0},{1,65},{65,1},{2,66},{66,2},{3,67},{67,3},{4,68},{68... | collective-permute-start | bytes 2359304 | tf_op jit(solution)/shard_map/ppermute | solution.py:354
  61.1 36.0 %collective-permute-start.2 = (bf16[128,1024]{1,0:T(8,128)(2,1)S(1)}, bf16[128,1024]{1,0:T(8,128)(2,1)}, u32[]{:S(2)}, u32[]{:S(2)}) collective-permute-start(bf16[128,1024]{1,0:T(8,128)(2,1)S(1)} %get-tuple-element.48), channel_id=1, source_target_pairs={{0,64},{64,0},{1,65},{65,1},{2,66},{66,2},{3,67},{67,3},{4,68},{68... | collective-permute-start | bytes 786440 | tf_op jit(solution)/shard_map/ppermute | solution.py:354

commit v3 on v2

--- a/solution.py
+++ b/solution.py
@@ -21,7 +21,7 @@
     for half,(own_ref,oth_ref) in enumerate(((own0,oth0),(own1,oth1))):
         def ln(i,_,half=half,own_ref=own_ref,oth_ref=oth_ref):
             r=pl.ds(pl.multiple_of(i*16,16),16)
-            o=pl.ds(pl.multiple_of(half*256+i*16,16),16)
+            o=pl.ds(pl.multiple_of(HEADCUT[half]+i*16,16),16)
             a=own_ref[r,:].astype(F); b=oth_ref[r,:].astype(F)
             m=jnp.sum(a+b,axis=1,keepdims=True)*(1.0/2048)
             a=a-m; b=b-m
@@ -30,7 +30,7 @@
             nrm[o,pl.ds(hoff,1024)]=(a*rs).astype(B)
             nrm[o,pl.ds(ooff,1024)]=(b*rs).astype(B)
             return 0
-        lax.fori_loop(0,16,ln,0,unroll=8)
+        lax.fori_loop(0,(HEADCUT[half+1]-HEADCUT[half])//16,ln,0,unroll=8)
     for c,dst,w in ((0,q,wq),(1,k,wk),(2,v,wv)):
         def proj(i,_,c=c,dst=dst,w=w):
             col=pl.ds(pl.multiple_of(i*256,256),256)
@@ -171,11 +171,11 @@
 def rows_unview(x):
     return x.reshape(512,8,4,128).transpose(0,2,1,3).reshape(512,4,1024)
 
-MR=256
-NCH=4
-TCH=MR//NCH
-
-def mix_body(base,r_ref,x_hbm,o_ref,x,sem):
+HEADCUT=(0,128,512)
+TCH=64
+
+def mix_body(base,size,r_ref,x_hbm,o_ref,x,sem):
+    NCH=size//TCH
     cps=[pltpu.make_async_copy(x_hbm.at[pl.ds(base*32+c*TCH*32,TCH*32),:],x.at[pl.ds(c*TCH*32,TCH*32),:],sem.at[c]) for c in range(NCH)]
     for c in cps: c.start()
     sh=(64,256); row=io(sh,0); col=io(sh,1)
@@ -194,26 +194,22 @@
                 o_ref[g*16:g*16+16,j*128:(j+1)*128]=jnp.concatenate([o[j*8:j*8+8,0:128],o[j*8:j*8+8,128:256]],axis=0).astype(B)
 
 def mix(i,x,r):
-    return pl.pallas_call(functools.partial(mix_body,i*MR),out_shape=jax.ShapeDtypeStruct((MR,1024),B),
+    base,MR=HEADCUT[i],HEADCUT[i+1]-HEADCUT[i]
+    return pl.pallas_call(functools.partial(mix_body,base,MR),out_shape=jax.ShapeDtypeStruct((MR,1024),B),
       in_specs=[pl.BlockSpec(memory_space=pltpu.SMEM),pl.BlockSpec(memory_space=pl.ANY)],
       out_specs=pl.BlockSpec(memory_space=pltpu.VMEM),
-      scratch_shapes=[pltpu.VMEM((MR*32,128),B),pltpu.SemaphoreType.DMA((NCH,))],
+      scratch_shapes=[pltpu.VMEM((MR*32,128),B),pltpu.SemaphoreType.DMA((MR//TCH,))],
       compiler_params=pltpu.CompilerParams(vmem_limit_bytes=61<<20),
       cost_estimate=pl.CostEstimate(flops=10**8,bytes_accessed=3<<20,transcendentals=0),
       name='mix')(r,x)
 
 CUTS=(0,384,512)
 NF=2
-STEP=64
-
-def fin_body(base,size,c_ref,w_ref,x_hbm,a_ref,b_ref,*rest):
-    o_hbm,x,o,m_ref,wm_ref,isem,osem=rest[-7:]
-    FCH=size//STEP
-    def span(c): return pl.ds((base+c*STEP)*32,STEP*32)
-    def part(c): return pl.ds(c*STEP*32,STEP*32)
-    icp=[pltpu.make_async_copy(x_hbm.at[span(c),:],x.at[part(c),:],isem.at[c]) for c in range(FCH)]
-    ocp=[pltpu.make_async_copy(o.at[part(c),:],o_hbm.at[span(c),:],osem.at[c]) for c in range(FCH)]
-    for c in icp: c.start()
+STEP=32
+
+def warm_body(c_ref,w_ref,x_hbm,x,m_ref,wm_ref,sem):
+    cp=pltpu.make_async_copy(x_hbm,x,sem)
+    cp.start()
     n=128
     row=io((n,n),0); col=io((n,n),1)
     a=jnp.zeros((n,n),F)
@@ -229,35 +225,48 @@
         a=jnp.where(((row>>5)+s*4==(col&7))&(((row>>2)&7)==(col>>3)),a,0.0)
         hi=a.astype(B); lo=(a-hi.astype(F)).astype(B)
         wm_ref[s*n:(s+1)*n,:]=jnp.concatenate([hi,lo,hi,lo],axis=1)
+    cp.wait()
+
+def warm(x,cr,w):
+    an=pl.BlockSpec(memory_space=pl.ANY); sm=pl.BlockSpec(memory_space=pltpu.SMEM); vm=pl.BlockSpec(memory_space=pltpu.VMEM)
+    return pl.pallas_call(warm_body,
+      out_shape=(jax.ShapeDtypeStruct((16384,128),B),jax.ShapeDtypeStruct((128,256),B),jax.ShapeDtypeStruct((256,256),B)),
+      in_specs=[sm,sm,an],out_specs=(vm,)*3,scratch_shapes=[pltpu.SemaphoreType.DMA],
+      compiler_params=pltpu.CompilerParams(vmem_limit_bytes=48<<20),
+      cost_estimate=pl.CostEstimate(flops=0,bytes_accessed=8<<20,transcendentals=0),
+      name='warm')(cr,w,x)
+
+def fin_body(base,size,x,m_ref,wm_ref,a_ref,b_ref,*rest):
+    o_hbm,o,osem=rest[-3:]
+    FCH=size//STEP
+    ocp=[pltpu.make_async_copy(o.at[pl.ds(c*STEP*32,STEP*32),:],o_hbm.at[pl.ds((base+c*STEP)*32,STEP*32),:],osem.at[c]) for c in range(FCH)]
     M=m_ref[...]
     for ch in range(FCH):
-        icp[ch].wait()
         for g in range(ch*STEP//16,(ch+1)*STEP//16):
             def U(ref):
                 u=ref[g*16:g*16+16,:].astype(F)
                 return jnp.concatenate([jnp.concatenate([u[0:8,j*128:(j+1)*128],u[8:16,j*128:(j+1)*128]],axis=1) for j in range(8)],axis=0).astype(B)
             Ua=U(a_ref);Ub=U(b_ref)
             ou=dot(wm_ref[...],jnp.concatenate([Ua,Ua,Ub,Ub],axis=0))
-            r0=g*512
+            r0=g*512; q0=base*32+r0
             for s in range(2):
-                X=jnp.concatenate([x[r0+s*128:r0+s*128+128,:],x[r0+256+s*128:r0+256+s*128+128,:]],axis=1)
+                X=jnp.concatenate([x[q0+s*128:q0+s*128+128,:],x[q0+256+s*128:q0+256+s*128+128,:]],axis=1)
                 z=(dot(M,jnp.concatenate([X,X],axis=0))+ou[s*128:(s+1)*128]).astype(B)
                 o[r0+s*128:r0+s*128+128,:]=z[:,0:128]; o[r0+256+s*128:r0+256+s*128+128,:]=z[:,128:256]
         ocp[ch].start()
     for c in ocp: c.wait()
 
-def fin(i,x,u1,u2,cr,w,prev):
-    an=pl.BlockSpec(memory_space=pl.ANY); sm=pl.BlockSpec(memory_space=pltpu.SMEM); vm=pl.BlockSpec(memory_space=pltpu.VMEM)
+def fin(i,ready,u1,u2,prev):
+    an=pl.BlockSpec(memory_space=pl.ANY); vm=pl.BlockSpec(memory_space=pltpu.VMEM)
     more=[] if prev is None else [prev]
     base,size=CUTS[i],CUTS[i+1]-CUTS[i]
     return pl.pallas_call(functools.partial(fin_body,base,size),out_shape=jax.ShapeDtypeStruct((16384,128),B),
-      in_specs=[sm,sm,an,vm,vm]+[an]*len(more),out_specs=an,
-      scratch_shapes=[pltpu.VMEM((size*32,128),B),pltpu.VMEM((size*32,128),B),pltpu.VMEM((128,256),B),pltpu.VMEM((256,256),B),
-        pltpu.SemaphoreType.DMA((size//STEP,)),pltpu.SemaphoreType.DMA((size//STEP,))],
+      in_specs=[vm]*5+[an]*len(more),out_specs=an,
+      scratch_shapes=[pltpu.VMEM((size*32,128),B),pltpu.SemaphoreType.DMA((size//STEP,))],
       input_output_aliases={5:0} if more else {},
-      compiler_params=pltpu.CompilerParams(vmem_limit_bytes=58<<20),
+      compiler_params=pltpu.CompilerParams(vmem_limit_bytes=16<<20),
       cost_estimate=pl.CostEstimate(flops=10**9*size//512,bytes_accessed=(10<<20)*size//512,transcendentals=0),
-      name='fin')(cr,w,x,u1,u2,*more)
+      name='fin')(*ready,u1,u2,*more)
 
 ROWS=2048
 PAY=2*ROWS+16
@@ -373,13 +382,15 @@
     r2=ahead(s2,2)
     q,k,v=proj(head,own0,own1,oth0,oth1,cos,sin,wq,wk,wv)
     parts=attn(lens,age,head,q,k,v,kc,vc,w_out)
-    keeps,sends=parts[:NF],parts[NF:]
+    keeps,sends=list(parts[:NF]),list(parts[NF:])
     recvs=[swap(s) for s in sends]
+    carry=(jnp.eye(4,dtype=F)+hc_carry).reshape(16)
+    xd,_=lax.optimization_barrier((x,keeps[0]))
+    ready=warm(xd,carry,hc_write)
     pages=place(page_table,me,pre,r1,r3,r2)
-    carry=(jnp.eye(4,dtype=F)+hc_carry).reshape(16)
-    recvs[0],pages=lax.optimization_barrier((recvs[0],pages))
+    ready,recvs[0],pages=lax.optimization_barrier((ready,recvs[0],pages))
     new=None
-    for i in range(NF): new=fin(i,x,keeps[i],recvs[i],carry,hc_write,new)
+    for i in range(NF): new=fin(i,ready,keeps[i],recvs[i],new)
     return rows_unview(new),tiles_unview(pages.reshape(8*ROWS,128)).reshape(8,1,2,128,1024)
 
 def solution(mesh):

time: 103 us -> 98.4 us (0.955); the launches traced: 101 us -> 97.5 us
  local copies, waits for them, and re-layouts: 2.28 us -> 0.13 us
  waiting for transfers between devices: 27.7 us -> 26 us
    pallas_call x2, Pallas kernels: 9.78 us -> 5.2 us  [fin(): pl.pallas_call(functools.partial(fin_body, base, size), out_shape=jax.Sha...]
    pallas_call x2 -> x3, Pallas kernels: 7.11 us -> 9.86 us  [the longest x2 7.11 us: mix(): pl.pallas_call(functools.partial(mix_body, base, MR), out_shape=jax.Shape...]
    ppermute x3, waiting for transfers between devices: 19.9 us -> 17.6 us  [ahead(): lax.ppermute(value, 'page', [(s, (s + steps) % 64) for s in range(64)])]
    pallas_call x1, Pallas kernels: 14.7 us -> 16.4 us  [attn(): pl.pallas_call(attn_body, out_shape=tuple((jax.ShapeDtypeStruct((CUTS[i +...]
    unnamed x20 -> x18, local copies, waits for them, and re-layouts: 1.61 us -> 0.05 us
  transfers between devices with their start and end apart: 7 -> 7, of which waited for: 3 -> 4; matrix products, arithmetic and copies ran while one was open for 2% -> 1% of each run, Pallas kernels for 50% -> 55%
where the time goes in v3:
time: 98.4 us; the launch traced here: 97.5 us
  Pallas kernels  57.7 us (59%)
  waiting for transfers between devices  26 us (26%)
  starting transfers between devices  11.4 us (12%)
  other arithmetic  1.28 us (1%)
  between operations  1 us (1%)
    ppermute x3, waiting for transfers between devices, ahead(): lax.ppermute(value, 'page', [(s, (s + steps) % 64) for s in range(64)])  17.6 us
    pallas_call x1, Pallas kernels, attn(): pl.pallas_call(attn_body, out_shape=tuple((jax.ShapeDtypeStruct((CUTS[i +...  16.4 us
    pallas_call x1, Pallas kernels, proj(): pl.pallas_call(proj_body, out_shape=(jax.ShapeDtypeStruct((512, 1024), B)...  12.2 us
    ppermute x4, waiting for transfers between devices, swap(): return lax.ppermute(value, 'head', [(0, 1), (1, 0)])  8.39 us
    ppermute x3, starting transfers between devices, ahead(): lax.ppermute(value, 'page', [(s, (s + steps) % 64) for s in range(64)])  7.64 us
    pallas_call x1, Pallas kernels, prep(): pl.pallas_call(prep_body, out_shape=tuple((jax.ShapeDtypeStruct(s, B) for...  7.16 us
    pallas_call x2, Pallas kernels, mix(): pl.pallas_call(functools.partial(mix_body, base, MR), out_shape=jax.Shape...  7.11 us
    pallas_call x2, Pallas kernels, fin(): pl.pallas_call(functools.partial(fin_body, base, size), out_shape=jax.Sha...  5.2 us
  transfers between devices with their start and end apart: 7, of which 4 were waited for; matrix products, arithmetic and copies ran while one was open for 1% of the time, Pallas kernels for 55%

profile of v3, /device:TPU:1, one launch (start us, length us, event | category | flops | bytes accessed | tf_op | source)
XLA Modules:
  0.0 97.5 jit_solution(796525629569169183)
XLA Ops:
  0.6 3.0 %mix.2.own0 = bf16[128,1024]{1,0:T(8,128)(2,1)} custom-call(f32[4]{0:T(128)} %r_ref.3, bf16[16384,128]{1,0:T(8,128)(2,1)} %bitcast.44), custom_call_target="tpu_custom_call" | custom-call | flops 100000000 | bytes 3145728 | tf_op jit(solution)/shard_map/mix/pallas_call | solution.py:198
  3.7 0.0 copy-start.6
  3.7 0.0 copy-start.7
  3.7 0.0 copy-start.4
  3.7 2.1 %collective-permute-start = (bf16[128,1024]{1,0:T(8,128)(2,1)}, bf16[128,1024]{1,0:T(8,128)(2,1)S(1)}, u32[]{:S(2)}, u32[]{:S(2)}) collective-permute-start(bf16[128,1024]{1,0:T(8,128)(2,1)} %mix.2.own0), channel_id=1, source_target_pairs={{0,64},{64,0},{1,65},{65,1},{2,66},{66,2},{3,67},{67,3},{4,68},{68... | collective-permute-start | bytes 786440 | tf_op jit(solution)/shard_map/ppermute | solution.py:363
  5.8 4.1 %mix.3.own1 = bf16[384,1024]{1,0:T(8,128)(2,1)} custom-call(f32[4]{0:T(128)} %r_ref.3, bf16[16384,128]{1,0:T(8,128)(2,1)} %bitcast.45), custom_call_target="tpu_custom_call" | custom-call | flops 100000000 | bytes 3145728 | tf_op jit(solution)/shard_map/mix/pallas_call | solution.py:198
  9.9 0.1 collective-permute-start.1
  10.1 2.5 %pick.1 = (bf16[4112,128]{1,0:T(8,128)(2,1)}, bf16[4112,128]{1,0:T(8,128)(2,1)}, bf16[4112,128]{1,0:T(8,128)(2,1)}) custom-call(s32[4]{0:T(128)S(1)} %copy-done.3, s32[1]{0:T(128)} %bitcast.8.me_ref, bf16[8192,128]{1,0:T(8,128)(2,1)S(1)} %bitcast.38), custom_call_target="tpu_custom_call" | custom-call | bytes 6291456 | tf_op jit(solution)/shard_map/pick/pallas_call | solution.py:308
  12.6 4.2 %collective-permute-start.3 = (bf16[4112,128]{1,0:T(8,128)(2,1)}, bf16[4112,128]{1,0:T(8,128)(2,1)}, u32[]{:S(2)}, u32[]{:S(2)}) collective-permute-start(bf16[4112,128]{1,0:T(8,128)(2,1)} %get-tuple-element.60), channel_id=1, source_target_pairs={{0,1},{1,2},{2,3},{3,4},{4,5},{5,6},{6,7},{7,8},{8,9},{9,10},{10,1... | collective-permute-start | bytes 3158024 | tf_op jit(solution)/shard_map/ppermute | solution.py:360
  16.7 0.0 collective-permute-start.4
  16.7 0.2 reduce-window.4
  16.9 0.1 select_reduce_fusion
  17.1 7.2 %prep.1 = (bf16[2048,1024]{1,0:T(8,128)(2,1)S(1)}, bf16[2048,1024]{1,0:T(8,128)(2,1)S(1)}, bf16[2048,1024]{1,0:T(8,128)(2,1)S(1)}, bf16[1536,1024]{1,0:T(8,128)(2,1)S(1)}, bf16[1536,1024]{1,0:T(8,128)(2,1)S(1)}) custom-call(s32[12]{0:T(128)S(1)} %bitcast.40, bf16[3,2048,1024]{2,1,0:T(8,128)(2,1)} %bitcast.48, bf16[12,2,128,1024]{3,2,1,0:T(8,128)(2,1)} %kv_hbm.1), custom_call_target="tpu_custom_call" | custom-call | bytes 48234496 | tf_op jit(solution)/shard_map/prep/pallas_call | solution.py:150
  24.2 1.0 %fusion = (f32[512,128]{1,0:T(8,128)S(1)}, f32[512,128]{1,0:T(8,128)S(1)}) fusion(f32[128]{0:T(128)S(1)} %get-tuple-element.74, f32[128]{0:T(128)S(1)} %get-tuple-element.75, f32[512]{0:T(512)S(1)} %add_convert_fusion), kind=kLoop, calls=%fused_computation.2 | loop fusion | flops 131072 | bytes 527360 | tf_op jit(solution)/shard_map/mul | solution.py:166
  25.2 3.2 %collective-permute-done.1.oth1 = bf16[384,1024]{1,0:T(8,128)(2,1)} collective-permute-done((bf16[384,1024]{1,0:T(8,128)(2,1)}, bf16[384,1024]{1,0:T(8,128)(2,1)}, u32[]{:S(2)}, u32[]{:S(2)}) %collective-permute-start.1) | collective-permute-done | bytes 786464 | tf_op jit(solution)/shard_map/ppermute | solution.py:363
  28.4 3.5 %collective-permute-start.5 = (bf16[4112,128]{1,0:T(8,128)(2,1)}, bf16[4112,128]{1,0:T(8,128)(2,1)}, u32[]{:S(2)}, u32[]{:S(2)}) collective-permute-start(bf16[4112,128]{1,0:T(8,128)(2,1)} %get-tuple-element.62), channel_id=1, source_target_pairs={{0,2},{1,3},{2,4},{3,5},{4,6},{5,7},{6,8},{7,9},{8,10},{9,11},{10,... | collective-permute-start | bytes 3158024 | tf_op jit(solution)/shard_map/ppermute | solution.py:360
  31.9 12.2 %proj.1 = (bf16[512,1024]{1,0:T(8,128)(2,1)S(1)}, bf16[512,1024]{1,0:T(8,128)(2,1)S(1)}, bf16[512,1024]{1,0:T(8,128)(2,1)S(1)}) custom-call(s32[1]{0:T(128)} %bitcast.5.head_ref, bf16[128,1024]{1,0:T(8,128)(2,1)S(1)} %copy-done.2, bf16[384,1024]{1,0:T(8,128)(2,1)S(1)} %copy-done.1, bf16[128,1024]{1,0:T(8,128)(2,1)S(1)} %collective-permute-done.oth0, ...), custom_call_target="tpu_custom_call" | custom-call | flops 7000000000 | bytes 16777216 | tf_op jit(solution)/shard_map/proj/pallas_call | solution.py:55
  44.1 0.0 copy-start.8
  44.1 0.0 copy-start.5
  44.2 16.4 %attn.1 = (bf16[384,1024]{1,0:T(8,128)(2,1)S(1)}, bf16[128,1024]{1,0:T(8,128)(2,1)S(1)}, bf16[384,1024]{1,0:T(8,128)(2,1)}, bf16[128,1024]{1,0:T(8,128)(2,1)}) custom-call(s32[4]{0:T(128)S(1)} %bitcast.42, s32[4]{0:T(128)S(1)} %bitcast.43, s32[1]{0:T(128)} %bitcast.5.head_ref, bf16[512,1024]{1,0:T(8,128)(2,1)S(1)} %get-tuple-element.49.q, ...), custom_call_target="tpu_custom_call" | custom-call | flops 7000000000 | bytes 16777216 | tf_op jit(solution)/shard_map/attn/pallas_call | solution.py:130
  60.5 0.5 collective-permute-start.2
  61.1 1.0 %collective-permute-start.6 = (bf16[128,1024]{1,0:T(8,128)(2,1)}, bf16[128,1024]{1,0:T(8,128)(2,1)S(1)}, u32[]{:S(2)}, u32[]{:S(2)}) collective-permute-start(bf16[128,1024]{1,0:T(8,128)(2,1)} %get-tuple-element.67), channel_id=1, source_target_pairs={{0,64},{64,0},{1,65},{65,1},{2,66},{66,2},{3,67},{67,3},{4,68},{68... | collective-permute-start | bytes 786440 | tf_op jit(solution)/shard_map/ppermute | solution.py:363
  62.1 0.1 reshape.65.c_ref
  62.2 2.7 %warm.1 = (bf16[16384,128]{1,0:T(8,128)(2,1)S(1)}, bf16[128,256]{1,0:T(8,128)(2,1)S(1)}, bf16[256,256]{1,0:T(8,128)(2,1)S(1)}) custom-call(f32[16]{0:T(128)S(1)} %reshape.65.c_ref, f32[4]{0:T(128)S(1)} %copy-done.5, bf16[16384,128]{1,0:T(8,128)(2,1)} %bitcast.46), custom_call_target="tpu_custom_call" | custom-call | bytes 8388608 | tf_op jit(solution)/shard_map/warm/pallas_call | solution.py:232
  64.9 0.0 collective-permute-done.3.r1
  65.0 0.0 collective-permute-done.4.r3
  65.0 17.6 %collective-permute-done.5.r2 = bf16[4112,128]{1,0:T(8,128)(2,1)} collective-permute-done((bf16[4112,128]{1,0:T(8,128)(2,1)}, bf16[4112,128]{1,0:T(8,128)(2,1)}, u32[]{:S(2)}, u32[]{:S(2)}) %collective-permute-start.5) | collective-permute-done | bytes 1052704 | tf_op jit(solution)/shard_map/ppermute | solution.py:360
  82.5 4.4 %place.1 = bf16[8,2048,128]{2,1,0:T(8,128)(2,1)} custom-call(s32[4]{0:T(128)S(1)} %copy-done.3, s32[1]{0:T(128)} %bitcast.8.me_ref, bf16[8192,128]{1,0:T(8,128)(2,1)S(1)} %bitcast.39, bf16[4112,128]{1,0:T(8,128)(2,1)} %collective-permute-done.3.r1, bf16[4112,128]{1,0:T(8,128)(2,1)} %collective-permute-done.4.r3, bf16[4112,128]{1,0:T(8,128)(2,1)} %collective-permute-done.5.r2), custom_call_target="tpu_custom_call" | custom-call | bytes 8388608 | tf_op jit(solution)/shard_map/place/pallas_call | solution.py:351
  87.0 3.4 %collective-permute-done.2.b_ref = bf16[384,1024]{1,0:T(8,128)(2,1)} collective-permute-done((bf16[384,1024]{1,0:T(8,128)(2,1)}, bf16[384,1024]{1,0:T(8,128)(2,1)}, u32[]{:S(2)}, u32[]{:S(2)}) %collective-permute-start.2) | collective-permute-done | bytes 786464 | tf_op jit(solution)/shard_map/ppermute | solution.py:363
  90.4 3.7 %fin.2.rest_0_ = bf16[16384,128]{1,0:T(8,128)(2,1)} custom-call(bf16[16384,128]{1,0:T(8,128)(2,1)S(1)} %get-tuple-element.63.x, bf16[128,256]{1,0:T(8,128)(2,1)S(1)} %get-tuple-element.64.m_ref, bf16[256,256]{1,0:T(8,128)(2,1)S(1)} %get-tuple-element.65.wm_ref, bf16[384,1024]{1,0:T(8,128)(2,1)S(1)} %get-tuple-element.54.a_ref, ...), custom_call_target="tpu_custom_call" | custom-call | flops 750000000 | bytes 7864320 | tf_op jit(solution)/shard_map/fin/pallas_call | solution.py:263
  94.1 1.8 %collective-permute-done.6.b_ref = bf16[128,1024]{1,0:T(8,128)(2,1)S(1)} collective-permute-done((bf16[128,1024]{1,0:T(8,128)(2,1)}, bf16[128,1024]{1,0:T(8,128)(2,1)S(1)}, u32[]{:S(2)}, u32[]{:S(2)}) %collective-permute-start.6) | collective-permute-done | bytes 262176 | tf_op jit(solution)/shard_map/ppermute | solution.py:363
  95.9 1.5 %fin.3 = bf16[16384,128]{1,0:T(8,128)(2,1)} custom-call(bf16[16384,128]{1,0:T(8,128)(2,1)S(1)} %get-tuple-element.63.x, bf16[128,256]{1,0:T(8,128)(2,1)S(1)} %get-tuple-element.64.m_ref, bf16[256,256]{1,0:T(8,128)(2,1)S(1)} %get-tuple-element.65.wm_ref, bf16[128,1024]{1,0:T(8,128)(2,1)S(1)} %get-tuple-element.66.a_ref, ...), custom_call_target="tpu_custom_call", output_to_operand_aliasing={{}: (5, {})} | custom-call | flops 250000000 | bytes 2621440 | tf_op jit(solution)/shard_map/fin/pallas_call | solution.py:263
  (18 shorter events, 0.1 us)
Async XLA Ops:
  0.6 9.4 %copy-start = (bf16[4,1,2,128,1024]{4,3,2,1,0:T(8,128)(2,1)S(1)}, bf16[4,1,2,128,1024]{4,3,2,1,0:T(8,128)(2,1)}, u32[]{:S(2)}) copy-start(bf16[4,1,2,128,1024]{4,3,2,1,0:T(8,128)(2,1)} %param.22) | copy-start | bytes 6291460
  0.6 9.4 %copy-start.3 = (s32[4]{0:T(128)S(1)}, s32[4]{0:T(128)}, u32[]{:S(2)}) copy-start(s32[4]{0:T(128)} %tab.1) | copy-start | bytes 52
  3.7 13.1 %copy-start.6 = (s32[1,4]{1,0:T(1,128)S(1)}, s32[1,4]{1,0:T(1,128)}, u32[]{:S(2)}) copy-start(s32[1,4]{1,0:T(1,128)} %param.18) | copy-start | bytes 52
  3.7 13.2 %copy-start.7 = (s32[1,4]{1,0:T(1,128)S(1)}, s32[1,4]{1,0:T(1,128)}, u32[]{:S(2)}) copy-start(s32[1,4]{1,0:T(1,128)} %param.19) | copy-start | bytes 52
  3.7 13.3 %copy-start.4 = (s32[1,12]{1,0:T(1,128)S(1)}, s32[1,12]{1,0:T(1,128)}, u32[]{:S(2)}) copy-start(s32[1,12]{1,0:T(1,128)} %param.20) | copy-start | bytes 148
  3.7 28.2 %collective-permute-start = (bf16[128,1024]{1,0:T(8,128)(2,1)}, bf16[128,1024]{1,0:T(8,128)(2,1)S(1)}, u32[]{:S(2)}, u32[]{:S(2)}) collective-permute-start(bf16[128,1024]{1,0:T(8,128)(2,1)} %mix.2.own0), channel_id=1, source_target_pairs={{0,64},{64,0},{1,65},{65,1},{2,66},{66,2},{3,67},{67,3},{4,68},{68... | collective-permute-start | bytes 786440 | tf_op jit(solution)/shard_map/ppermute | solution.py:363
  9.9 18.5 %collective-permute-start.1 = (bf16[384,1024]{1,0:T(8,128)(2,1)}, bf16[384,1024]{1,0:T(8,128)(2,1)}, u32[]{:S(2)}, u32[]{:S(2)}) collective-permute-start(bf16[384,1024]{1,0:T(8,128)(2,1)} %mix.3.own1), channel_id=1, source_target_pairs={{0,64},{64,0},{1,65},{65,1},{2,66},{66,2},{3,67},{67,3},{4,68},{68... | collective-permute-start | bytes 2359304 | tf_op jit(solution)/shard_map/ppermute | solution.py:363
  12.6 52.4 %collective-permute-start.3 = (bf16[4112,128]{1,0:T(8,128)(2,1)}, bf16[4112,128]{1,0:T(8,128)(2,1)}, u32[]{:S(2)}, u32[]{:S(2)}) collective-permute-start(bf16[4112,128]{1,0:T(8,128)(2,1)} %get-tuple-element.60), channel_id=1, source_target_pairs={{0,1},{1,2},{2,3},{3,4},{4,5},{5,6},{6,7},{7,8},{8,9},{9,10},{10,1... | collective-permute-start | bytes 3158024 | tf_op jit(solution)/shard_map/ppermute | solution.py:360
  16.7 48.2 %collective-permute-start.4 = (bf16[4112,128]{1,0:T(8,128)(2,1)}, bf16[4112,128]{1,0:T(8,128)(2,1)}, u32[]{:S(2)}, u32[]{:S(2)}) collective-permute-start(bf16[4112,128]{1,0:T(8,128)(2,1)} %get-tuple-element.61), channel_id=1, source_target_pairs={{0,3},{1,4},{2,5},{3,6},{4,7},{5,8},{6,9},{7,10},{8,11},{9,12},{10... | collective-permute-start | bytes 3158024 | tf_op jit(solution)/shard_map/ppermute | solution.py:360
  17.0 14.9 %copy-start.1 = (bf16[384,1024]{1,0:T(8,128)(2,1)S(1)}, bf16[384,1024]{1,0:T(8,128)(2,1)}, u32[]{:S(2)}) copy-start(bf16[384,1024]{1,0:T(8,128)(2,1)} %mix.3.own1) | copy-start | bytes 2359300
  17.0 14.9 %copy-start.2 = (bf16[128,1024]{1,0:T(8,128)(2,1)S(1)}, bf16[128,1024]{1,0:T(8,128)(2,1)}, u32[]{:S(2)}) copy-start(bf16[128,1024]{1,0:T(8,128)(2,1)} %mix.2.own0) | copy-start | bytes 786436
  28.4 54.1 %collective-permute-start.5 = (bf16[4112,128]{1,0:T(8,128)(2,1)}, bf16[4112,128]{1,0:T(8,128)(2,1)}, u32[]{:S(2)}, u32[]{:S(2)}) collective-permute-start(bf16[4112,128]{1,0:T(8,128)(2,1)} %get-tuple-element.62), channel_id=1, source_target_pairs={{0,2},{1,3},{2,4},{3,5},{4,6},{5,7},{6,8},{7,9},{8,10},{9,11},{10,... | collective-permute-start | bytes 3158024 | tf_op jit(solution)/shard_map/ppermute | solution.py:360
  44.1 18.0 %copy-start.8 = (f32[4,4]{1,0:T(4,128)S(1)}, f32[4,4]{1,0:T(4,128)}, u32[]{:S(2)}) copy-start(f32[4,4]{1,0:T(4,128)} %param.14) | copy-start | bytes 196
  44.1 18.0 %copy-start.5 = (f32[4]{0:T(128)S(1)}, f32[4]{0:T(128)}, u32[]{:S(2)}) copy-start(f32[4]{0:T(128)} %w_ref.1) | copy-start | bytes 52
  60.5 29.8 %collective-permute-start.2 = (bf16[384,1024]{1,0:T(8,128)(2,1)}, bf16[384,1024]{1,0:T(8,128)(2,1)}, u32[]{:S(2)}, u32[]{:S(2)}) collective-permute-start(bf16[384,1024]{1,0:T(8,128)(2,1)} %get-tuple-element.59), channel_id=1, source_target_pairs={{0,64},{64,0},{1,65},{65,1},{2,66},{66,2},{3,67},{67,3},{4,68},{68... | collective-permute-start | bytes 2359304 | tf_op jit(solution)/shard_map/ppermute | solution.py:363
  61.1 34.8 %collective-permute-start.6 = (bf16[128,1024]{1,0:T(8,128)(2,1)}, bf16[128,1024]{1,0:T(8,128)(2,1)S(1)}, u32[]{:S(2)}, u32[]{:S(2)}) collective-permute-start(bf16[128,1024]{1,0:T(8,128)(2,1)} %get-tuple-element.67), channel_id=1, source_target_pairs={{0,64},{64,0},{1,65},{65,1},{2,66},{66,2},{3,67},{67,3},{4,68},{68... | collective-permute-start | bytes 786440 | tf_op jit(solution)/shard_map/ppermute | solution.py:363

commit v4 on v3

--- a/solution.py
+++ b/solution.py
@@ -375,11 +375,10 @@
     pre=tiles_view(prefill_kv.reshape(1024,1024))
     own_dep,table=lax.optimization_barrier((own1,page_table))
     s1,s2,s3=pick(table,me,pre)
-    r3=ahead(s3,3); r1=ahead(s1,1)
+    r2=ahead(s2,2); r3=ahead(s3,3); r1=ahead(s1,1)
     cos,sin=tables(lens,age)
     wq,wk,wv,kc,vc=prep(order,w_qkv.transpose(1,0,2),cache_kv)
-    oth1,s2,wq,wk,wv,kc,vc=lax.optimization_barrier((oth1,s2,wq,wk,wv,kc,vc))
-    r2=ahead(s2,2)
+    oth1,wq,wk,wv,kc,vc=lax.optimization_barrier((oth1,wq,wk,wv,kc,vc))
     q,k,v=proj(head,own0,own1,oth0,oth1,cos,sin,wq,wk,wv)
     parts=attn(lens,age,head,q,k,v,kc,vc,w_out)
     keeps,sends=list(parts[:NF]),list(parts[NF:])

time: 98.4 us -> 99.5 us (1.011)
  waiting for transfers between devices: 26 us -> 28.7 us
  starting transfers between devices: 11.4 us -> 9.69 us
    ppermute x3, waiting for transfers between devices: 17.6 us -> 21.5 us  [ahead(): lax.ppermute(value, 'page', [(s, (s + steps) % 64) for s in range(64)])]
    ppermute x3, starting transfers between devices: 7.64 us -> 5.53 us  [ahead(): lax.ppermute(value, 'page', [(s, (s + steps) % 64) for s in range(64)])]
    ppermute x4, waiting for transfers between devices: 8.39 us -> 7.18 us  [swap(): return lax.ppermute(value, 'head', [(0, 1), (1, 0)])]
  transfers between devices with their start and end apart: 7 -> 7, of which waited for: 4 -> 5; matrix products, arithmetic and copies ran while one was open for 1% -> 1% of each run, Pallas kernels for 55% -> 53%
where the time goes in v4:
time: 99.5 us; the launch traced here: 98.6 us
  Pallas kernels  57.8 us (58%)
  waiting for transfers between devices  28.7 us (29%)
  starting transfers between devices  9.69 us (10%)
  other arithmetic  1.28 us (1%)
    ppermute x3, waiting for transfers between devices, ahead(): lax.ppermute(value, 'page', [(s, (s + steps) % 64) for s in range(64)])  21.5 us
    pallas_call x1, Pallas kernels, attn(): pl.pallas_call(attn_body, out_shape=tuple((jax.ShapeDtypeStruct((CUTS[i +...  15.5 us
    pallas_call x1, Pallas kernels, proj(): pl.pallas_call(proj_body, out_shape=(jax.ShapeDtypeStruct((512, 1024), B)...  12.2 us
    ppermute x4, waiting for transfers between devices, swap(): return lax.ppermute(value, 'head', [(0, 1), (1, 0)])  7.18 us
    pallas_call x1, Pallas kernels, prep(): pl.pallas_call(prep_body, out_shape=tuple((jax.ShapeDtypeStruct(s, B) for...  7.16 us
    pallas_call x2, Pallas kernels, mix(): pl.pallas_call(functools.partial(mix_body, base, MR), out_shape=jax.Shape...  7.11 us
    pallas_call x2, Pallas kernels, fin(): pl.pallas_call(functools.partial(fin_body, base, size), out_shape=jax.Sha...  6.14 us
    ppermute x3, starting transfers between devices, ahead(): lax.ppermute(value, 'page', [(s, (s + steps) % 64) for s in range(64)])  5.53 us
  transfers between devices with their start and end apart: 7, of which 5 were waited for; matrix products, arithmetic and copies ran while one was open for 1% of the time, Pallas kernels for 53%

profile of v4, /device:TPU:1, one launch (start us, length us, event | category | flops | bytes accessed | tf_op | source)
XLA Modules:
  0.0 98.6 jit_solution(4991990910184247531)
XLA Ops:
  0.6 3.0 %mix.2.own0 = bf16[128,1024]{1,0:T(8,128)(2,1)} custom-call(f32[4]{0:T(128)} %r_ref.3, bf16[16384,128]{1,0:T(8,128)(2,1)} %bitcast.44), custom_call_target="tpu_custom_call" | custom-call | flops 100000000 | bytes 3145728 | tf_op jit(solution)/shard_map/mix/pallas_call | solution.py:198
  3.7 0.0 copy-start.6
  3.7 0.0 copy-start.7
  3.7 0.0 copy-start.4
  3.7 2.1 %collective-permute-start = (bf16[128,1024]{1,0:T(8,128)(2,1)}, bf16[128,1024]{1,0:T(8,128)(2,1)S(1)}, u32[]{:S(2)}, u32[]{:S(2)}) collective-permute-start(bf16[128,1024]{1,0:T(8,128)(2,1)} %mix.2.own0), channel_id=1, source_target_pairs={{0,64},{64,0},{1,65},{65,1},{2,66},{66,2},{3,67},{67,3},{4,68},{68... | collective-permute-start | bytes 786440 | tf_op jit(solution)/shard_map/ppermute | solution.py:363
  5.8 4.1 %mix.3.own1 = bf16[384,1024]{1,0:T(8,128)(2,1)} custom-call(f32[4]{0:T(128)} %r_ref.3, bf16[16384,128]{1,0:T(8,128)(2,1)} %bitcast.45), custom_call_target="tpu_custom_call" | custom-call | flops 100000000 | bytes 3145728 | tf_op jit(solution)/shard_map/mix/pallas_call | solution.py:198
  9.9 0.1 collective-permute-start.1
  10.1 2.5 %pick.1 = (bf16[4112,128]{1,0:T(8,128)(2,1)}, bf16[4112,128]{1,0:T(8,128)(2,1)}, bf16[4112,128]{1,0:T(8,128)(2,1)}) custom-call(s32[4]{0:T(128)S(1)} %copy-done.3, s32[1]{0:T(128)} %bitcast.15.me_ref, bf16[8192,128]{1,0:T(8,128)(2,1)S(1)} %bitcast.38), custom_call_target="tpu_custom_call" | custom-call | bytes 6291456 | tf_op jit(solution)/shard_map/pick/pallas_call | solution.py:308
  12.6 4.2 %collective-permute-start.3 = (bf16[4112,128]{1,0:T(8,128)(2,1)}, bf16[4112,128]{1,0:T(8,128)(2,1)}, u32[]{:S(2)}, u32[]{:S(2)}) collective-permute-start(bf16[4112,128]{1,0:T(8,128)(2,1)} %get-tuple-element.58), channel_id=1, source_target_pairs={{0,1},{1,2},{2,3},{3,4},{4,5},{5,6},{6,7},{7,8},{8,9},{9,10},{10,1... | collective-permute-start | bytes 3158024 | tf_op jit(solution)/shard_map/ppermute | solution.py:360
  16.7 0.0 collective-permute-start.4
  16.7 1.4 %collective-permute-start.5 = (bf16[4112,128]{1,0:T(8,128)(2,1)}, bf16[4112,128]{1,0:T(8,128)(2,1)}, u32[]{:S(2)}, u32[]{:S(2)}) collective-permute-start(bf16[4112,128]{1,0:T(8,128)(2,1)} %get-tuple-element.60), channel_id=1, source_target_pairs={{0,2},{1,3},{2,4},{3,5},{4,6},{5,7},{6,8},{7,9},{8,10},{9,11},{10,... | collective-permute-start | bytes 3158024 | tf_op jit(solution)/shard_map/ppermute | solution.py:360
  18.1 0.2 reduce-window.4
  18.3 0.1 select_reduce_fusion
  18.4 7.2 %prep.1 = (bf16[2048,1024]{1,0:T(8,128)(2,1)S(1)}, bf16[2048,1024]{1,0:T(8,128)(2,1)S(1)}, bf16[2048,1024]{1,0:T(8,128)(2,1)S(1)}, bf16[1536,1024]{1,0:T(8,128)(2,1)S(1)}, bf16[1536,1024]{1,0:T(8,128)(2,1)S(1)}) custom-call(s32[12]{0:T(128)S(1)} %bitcast.40, bf16[3,2048,1024]{2,1,0:T(8,128)(2,1)} %bitcast.48, bf16[12,2,128,1024]{3,2,1,0:T(8,128)(2,1)} %kv_hbm.1), custom_call_target="tpu_custom_call" | custom-call | bytes 48234496 | tf_op jit(solution)/shard_map/prep/pallas_call | solution.py:150
  25.6 1.0 %fusion = (f32[512,128]{1,0:T(8,128)S(1)}, f32[512,128]{1,0:T(8,128)S(1)}) fusion(f32[128]{0:T(128)S(1)} %get-tuple-element.72, f32[128]{0:T(128)S(1)} %get-tuple-element.73, f32[512]{0:T(512)S(1)} %add_convert_fusion), kind=kLoop, calls=%fused_computation.2 | loop fusion | flops 131072 | bytes 527360 | tf_op jit(solution)/shard_map/mul | solution.py:166
  26.6 1.8 %collective-permute-done.1.oth1 = bf16[384,1024]{1,0:T(8,128)(2,1)} collective-permute-done((bf16[384,1024]{1,0:T(8,128)(2,1)}, bf16[384,1024]{1,0:T(8,128)(2,1)}, u32[]{:S(2)}, u32[]{:S(2)}) %collective-permute-start.1) | collective-permute-done | bytes 786464 | tf_op jit(solution)/shard_map/ppermute | solution.py:363
  28.4 12.2 %proj.1 = (bf16[512,1024]{1,0:T(8,128)(2,1)S(1)}, bf16[512,1024]{1,0:T(8,128)(2,1)S(1)}, bf16[512,1024]{1,0:T(8,128)(2,1)S(1)}) custom-call(s32[1]{0:T(128)} %bitcast.5.head_ref, bf16[128,1024]{1,0:T(8,128)(2,1)S(1)} %copy-done.2, bf16[384,1024]{1,0:T(8,128)(2,1)S(1)} %copy-done.1, bf16[128,1024]{1,0:T(8,128)(2,1)S(1)} %collective-permute-done.oth0, ...), custom_call_target="tpu_custom_call" | custom-call | flops 7000000000 | bytes 16777216 | tf_op jit(solution)/shard_map/proj/pallas_call | solution.py:55
  40.6 0.0 copy-start.8
  40.7 0.0 copy-start.5
  40.7 15.5 %attn.1 = (bf16[384,1024]{1,0:T(8,128)(2,1)S(1)}, bf16[128,1024]{1,0:T(8,128)(2,1)S(1)}, bf16[384,1024]{1,0:T(8,128)(2,1)}, bf16[128,1024]{1,0:T(8,128)(2,1)}) custom-call(s32[4]{0:T(128)S(1)} %bitcast.42, s32[4]{0:T(128)S(1)} %bitcast.43, s32[1]{0:T(128)} %bitcast.5.head_ref, bf16[512,1024]{1,0:T(8,128)(2,1)S(1)} %get-tuple-element.46.q, ...), custom_call_target="tpu_custom_call" | custom-call | flops 7000000000 | bytes 16777216 | tf_op jit(solution)/shard_map/attn/pallas_call | solution.py:130
  56.2 1.8 %collective-permute-start.2 = (bf16[384,1024]{1,0:T(8,128)(2,1)}, bf16[384,1024]{1,0:T(8,128)(2,1)}, u32[]{:S(2)}, u32[]{:S(2)}) collective-permute-start(bf16[384,1024]{1,0:T(8,128)(2,1)} %get-tuple-element.56), channel_id=1, source_target_pairs={{0,64},{64,0},{1,65},{65,1},{2,66},{66,2},{3,67},{67,3},{4,68},{68... | collective-permute-start | bytes 2359304 | tf_op jit(solution)/shard_map/ppermute | solution.py:363
  58.0 0.1 collective-permute-start.6
  58.1 0.1 reshape.65.c_ref
  58.2 2.7 %warm.1 = (bf16[16384,128]{1,0:T(8,128)(2,1)S(1)}, bf16[128,256]{1,0:T(8,128)(2,1)S(1)}, bf16[256,256]{1,0:T(8,128)(2,1)S(1)}) custom-call(f32[16]{0:T(128)S(1)} %reshape.65.c_ref, f32[4]{0:T(128)S(1)} %copy-done.5, bf16[16384,128]{1,0:T(8,128)(2,1)} %bitcast.46), custom_call_target="tpu_custom_call" | custom-call | bytes 8388608 | tf_op jit(solution)/shard_map/warm/pallas_call | solution.py:232
  61.0 0.0 collective-permute-done.3.r1
  61.0 0.3 collective-permute-done.4.r3
  61.3 21.2 %collective-permute-done.5.r2 = bf16[4112,128]{1,0:T(8,128)(2,1)} collective-permute-done((bf16[4112,128]{1,0:T(8,128)(2,1)}, bf16[4112,128]{1,0:T(8,128)(2,1)}, u32[]{:S(2)}, u32[]{:S(2)}) %collective-permute-start.5) | collective-permute-done | bytes 1052704 | tf_op jit(solution)/shard_map/ppermute | solution.py:360
  82.5 4.4 %place.1 = bf16[8,2048,128]{2,1,0:T(8,128)(2,1)} custom-call(s32[4]{0:T(128)S(1)} %copy-done.3, s32[1]{0:T(128)} %bitcast.15.me_ref, bf16[8192,128]{1,0:T(8,128)(2,1)S(1)} %bitcast.39, bf16[4112,128]{1,0:T(8,128)(2,1)} %collective-permute-done.3.r1, bf16[4112,128]{1,0:T(8,128)(2,1)} %collective-permute-done.4.r3, bf16[4112,128]{1,0:T(8,128)(2,1)} %collective-permute-done.5.r2), custom_call_target="tpu_custom_call" | custom-call | bytes 8388608 | tf_op jit(solution)/shard_map/place/pallas_call | solution.py:351
  86.9 3.5 %collective-permute-done.2.b_ref = bf16[384,1024]{1,0:T(8,128)(2,1)} collective-permute-done((bf16[384,1024]{1,0:T(8,128)(2,1)}, bf16[384,1024]{1,0:T(8,128)(2,1)}, u32[]{:S(2)}, u32[]{:S(2)}) %collective-permute-start.2) | collective-permute-done | bytes 786464 | tf_op jit(solution)/shard_map/ppermute | solution.py:363
  90.4 3.7 %fin.2.rest_0_ = bf16[16384,128]{1,0:T(8,128)(2,1)} custom-call(bf16[16384,128]{1,0:T(8,128)(2,1)S(1)} %get-tuple-element.61.x, bf16[128,256]{1,0:T(8,128)(2,1)S(1)} %get-tuple-element.62.m_ref, bf16[256,256]{1,0:T(8,128)(2,1)S(1)} %get-tuple-element.63.wm_ref, bf16[384,1024]{1,0:T(8,128)(2,1)S(1)} %get-tuple-element.51.a_ref, ...), custom_call_target="tpu_custom_call" | custom-call | flops 750000000 | bytes 7864320 | tf_op jit(solution)/shard_map/fin/pallas_call | solution.py:263
  94.1 1.9 %collective-permute-done.6.b_ref = bf16[128,1024]{1,0:T(8,128)(2,1)} collective-permute-done((bf16[128,1024]{1,0:T(8,128)(2,1)}, bf16[128,1024]{1,0:T(8,128)(2,1)}, u32[]{:S(2)}, u32[]{:S(2)}) %collective-permute-start.6) | collective-permute-done | bytes 262176 | tf_op jit(solution)/shard_map/ppermute | solution.py:363
  96.0 2.4 %fin.3 = bf16[16384,128]{1,0:T(8,128)(2,1)} custom-call(bf16[16384,128]{1,0:T(8,128)(2,1)S(1)} %get-tuple-element.61.x, bf16[128,256]{1,0:T(8,128)(2,1)S(1)} %get-tuple-element.62.m_ref, bf16[256,256]{1,0:T(8,128)(2,1)S(1)} %get-tuple-element.63.wm_ref, bf16[128,1024]{1,0:T(8,128)(2,1)S(1)} %get-tuple-element.64.a_ref, ...), custom_call_target="tpu_custom_call", output_to_operand_aliasing={{}: (5, {})} | custom-call | flops 250000000 | bytes 2621440 | tf_op jit(solution)/shard_map/fin/pallas_call | solution.py:263
  (18 shorter events, 0.1 us)
Async XLA Ops:
  0.6 9.4 %copy-start = (bf16[4,1,2,128,1024]{4,3,2,1,0:T(8,128)(2,1)S(1)}, bf16[4,1,2,128,1024]{4,3,2,1,0:T(8,128)(2,1)}, u32[]{:S(2)}) copy-start(bf16[4,1,2,128,1024]{4,3,2,1,0:T(8,128)(2,1)} %param.22) | copy-start | bytes 6291460
  0.6 9.4 %copy-start.3 = (s32[4]{0:T(128)S(1)}, s32[4]{0:T(128)}, u32[]{:S(2)}) copy-start(s32[4]{0:T(128)} %tab.1) | copy-start | bytes 52
  3.7 14.4 %copy-start.6 = (s32[1,4]{1,0:T(1,128)S(1)}, s32[1,4]{1,0:T(1,128)}, u32[]{:S(2)}) copy-start(s32[1,4]{1,0:T(1,128)} %param.18) | copy-start | bytes 52
  3.7 14.6 %copy-start.7 = (s32[1,4]{1,0:T(1,128)S(1)}, s32[1,4]{1,0:T(1,128)}, u32[]{:S(2)}) copy-start(s32[1,4]{1,0:T(1,128)} %param.19) | copy-start | bytes 52
  3.7 14.7 %copy-start.4 = (s32[1,12]{1,0:T(1,128)S(1)}, s32[1,12]{1,0:T(1,128)}, u32[]{:S(2)}) copy-start(s32[1,12]{1,0:T(1,128)} %param.20) | copy-start | bytes 148
  3.7 24.7 %collective-permute-start = (bf16[128,1024]{1,0:T(8,128)(2,1)}, bf16[128,1024]{1,0:T(8,128)(2,1)S(1)}, u32[]{:S(2)}, u32[]{:S(2)}) collective-permute-start(bf16[128,1024]{1,0:T(8,128)(2,1)} %mix.2.own0), channel_id=1, source_target_pairs={{0,64},{64,0},{1,65},{65,1},{2,66},{66,2},{3,67},{67,3},{4,68},{68... | collective-permute-start | bytes 786440 | tf_op jit(solution)/shard_map/ppermute | solution.py:363
  9.9 18.5 %collective-permute-start.1 = (bf16[384,1024]{1,0:T(8,128)(2,1)}, bf16[384,1024]{1,0:T(8,128)(2,1)}, u32[]{:S(2)}, u32[]{:S(2)}) collective-permute-start(bf16[384,1024]{1,0:T(8,128)(2,1)} %mix.3.own1), channel_id=1, source_target_pairs={{0,64},{64,0},{1,65},{65,1},{2,66},{66,2},{3,67},{67,3},{4,68},{68... | collective-permute-start | bytes 2359304 | tf_op jit(solution)/shard_map/ppermute | solution.py:363
  12.6 48.4 %collective-permute-start.3 = (bf16[4112,128]{1,0:T(8,128)(2,1)}, bf16[4112,128]{1,0:T(8,128)(2,1)}, u32[]{:S(2)}, u32[]{:S(2)}) collective-permute-start(bf16[4112,128]{1,0:T(8,128)(2,1)} %get-tuple-element.58), channel_id=1, source_target_pairs={{0,1},{1,2},{2,3},{3,4},{4,5},{5,6},{6,7},{7,8},{8,9},{9,10},{10,1... | collective-permute-start | bytes 3158024 | tf_op jit(solution)/shard_map/ppermute | solution.py:360
  16.7 44.6 %collective-permute-start.4 = (bf16[4112,128]{1,0:T(8,128)(2,1)}, bf16[4112,128]{1,0:T(8,128)(2,1)}, u32[]{:S(2)}, u32[]{:S(2)}) collective-permute-start(bf16[4112,128]{1,0:T(8,128)(2,1)} %get-tuple-element.59), channel_id=1, source_target_pairs={{0,3},{1,4},{2,5},{3,6},{4,7},{5,8},{6,9},{7,10},{8,11},{9,12},{10... | collective-permute-start | bytes 3158024 | tf_op jit(solution)/shard_map/ppermute | solution.py:360
  16.7 65.8 %collective-permute-start.5 = (bf16[4112,128]{1,0:T(8,128)(2,1)}, bf16[4112,128]{1,0:T(8,128)(2,1)}, u32[]{:S(2)}, u32[]{:S(2)}) collective-permute-start(bf16[4112,128]{1,0:T(8,128)(2,1)} %get-tuple-element.60), channel_id=1, source_target_pairs={{0,2},{1,3},{2,4},{3,5},{4,6},{5,7},{6,8},{7,9},{8,10},{9,11},{10,... | collective-permute-start | bytes 3158024 | tf_op jit(solution)/shard_map/ppermute | solution.py:360
  18.4 10.0 %copy-start.1 = (bf16[384,1024]{1,0:T(8,128)(2,1)S(1)}, bf16[384,1024]{1,0:T(8,128)(2,1)}, u32[]{:S(2)}) copy-start(bf16[384,1024]{1,0:T(8,128)(2,1)} %mix.3.own1) | copy-start | bytes 2359300
  18.4 10.0 %copy-start.2 = (bf16[128,1024]{1,0:T(8,128)(2,1)S(1)}, bf16[128,1024]{1,0:T(8,128)(2,1)}, u32[]{:S(2)}) copy-start(bf16[128,1024]{1,0:T(8,128)(2,1)} %mix.2.own0) | copy-start | bytes 786436
  40.6 17.5 %copy-start.8 = (f32[4,4]{1,0:T(4,128)S(1)}, f32[4,4]{1,0:T(4,128)}, u32[]{:S(2)}) copy-start(f32[4,4]{1,0:T(4,128)} %param.14) | copy-start | bytes 196
  40.7 17.6 %copy-start.5 = (f32[4]{0:T(128)S(1)}, f32[4]{0:T(128)}, u32[]{:S(2)}) copy-start(f32[4]{0:T(128)} %w_ref.1) | copy-start | bytes 52
  56.2 34.2 %collective-permute-start.2 = (bf16[384,1024]{1,0:T(8,128)(2,1)}, bf16[384,1024]{1,0:T(8,128)(2,1)}, u32[]{:S(2)}, u32[]{:S(2)}) collective-permute-start(bf16[384,1024]{1,0:T(8,128)(2,1)} %get-tuple-element.56), channel_id=1, source_target_pairs={{0,64},{64,0},{1,65},{65,1},{2,66},{66,2},{3,67},{67,3},{4,68},{68... | collective-permute-start | bytes 2359304 | tf_op jit(solution)/shard_map/ppermute | solution.py:363
  58.0 38.0 %collective-permute-start.6 = (bf16[128,1024]{1,0:T(8,128)(2,1)}, bf16[128,1024]{1,0:T(8,128)(2,1)}, u32[]{:S(2)}, u32[]{:S(2)}) collective-permute-start(bf16[128,1024]{1,0:T(8,128)(2,1)} %get-tuple-element.65), channel_id=1, source_target_pairs={{0,64},{64,0},{1,65},{65,1},{2,66},{66,2},{3,67},{67,3},{4,68},{68... | collective-permute-start | bytes 786440 | tf_op jit(solution)/shard_map/ppermute | solution.py:363
